TPU v7x, 128 devices: a whole 4x4x4 slice. The times are simulated.
128 devices in a mesh: gx: 8 (over z, x_hi), yz: 16 (over y, x_lo, core).
Axes of the slice: x: 4 (x_hi: 2, x_lo: 2; x = x_hi * 2 + x_lo), y: 4, z: 4, core: 2. Of those that a mesh axis runs over, the one named last changes fastest.
Arguments:
- features: bfloat16 [65536, 128], P(('gx', 'yz')), may hold values from -6 to 6
- frac: float32 [3, 65536], P(None, ('gx', 'yz')), may hold values from 0 to 1
- neighbours: int32 [32, 65536], P(None, ('gx', 'yz')), may hold values from 0 to 2815
- nbr_mask: int32 [32, 65536], P(None, ('gx', 'yz')), may hold values 0 or 1
- send_list: int32 [32768], P(('gx', 'yz')), may hold values from 0 to 511
- wavevectors: int32 [3, 4096], P(None, ('gx', 'yz')), may hold values from -6 to 6
- w_in: bfloat16 [2, 128, 128], replicated, may hold values from -0.5 to 0.5
- w_filter1: bfloat16 [2, 32, 128], replicated, may hold values from -2 to 2
- w_filter2: bfloat16 [2, 128, 128], replicated, may hold values from -0.5 to 0.5
- w_update1: bfloat16 [2, 128, 128], replicated, may hold values from -0.5 to 0.5
- w_update2: bfloat16 [2, 128, 128], replicated, may hold values from -0.5 to 0.5
- w_charge: bfloat16 [128, 16], replicated, may hold values from -0.5 to 0.5
- screening: float32 [16], replicated, may hold values from 1 to 64
- w_head: bfloat16 [128, 128], replicated, may hold values from -0.5 to 0.5
- w_potential: bfloat16 [16, 128], replicated, may hold values from -1.5 to 1.5
- w_energy: bfloat16 [128], replicated, may hold values from -0.5 to 0.5
Outputs:
- embeddings: bfloat16 [65536, 128], P(('gx', 'yz'))
- potentials: float32 [16, 65536], P(None, ('gx', 'yz'))
- energies: float32 [65536], P(('gx', 'yz'))
All inputs are finite; a program needn't handle non-finite values. No bound on the sum of `nbr_mask` on one device may be relied on, other than what follows from the above.
Results may differ from a plain program's by a relative error of at most 0.025.
Values may be sent and summed in bfloat16 or wider, within the bound.
No kernel may reach another device: no remote copies, remote signals or barrier semaphores. Data moves between devices by JAX's collectives and lax.ppermute only.
A program may use at most 64 MiB of HBM per device.

v0:
```python
import math

import jax
import jax.numpy as jnp
from jax import lax
from jax.sharding import PartitionSpec as P

C = 128
NR = 32
Q = 16
MODES = 4096
K = 32
LAYERS = 2
HALO_SIDE = 16
ATOMS_DEV = 512
HALO_DEV = 256


two_pi = 2.0 * math.pi
ewald_width = 64.0


def with_halo(block, sides, width):
    for axis, dim in sides:
        count = lax.axis_size(axis)
        forward = [(i, i + 1) for i in range(count - 1)]
        forward.append((count - 1, 0))
        backward = [(target, source) for source, target in forward]
        low = lax.ppermute(
            lax.slice_in_dim(block, block.shape[dim] - width, None, axis=dim), axis, forward
        )
        high = lax.ppermute(lax.slice_in_dim(block, 0, width, axis=dim), axis, backward)
        block = jnp.concatenate([low, block, high], axis=dim)
    return block


def radial_basis(chord_sq, basis_count):
    spacing = 3.0 / (basis_count - 1)
    centres = jnp.arange(basis_count, dtype=jnp.float32) * spacing
    scaled = (chord_sq[..., None] - centres) / spacing
    return jnp.exp(-0.5 * scaled * scaled).astype(jnp.bfloat16)


def mode_phases(coords, wave_block):
    angles = two_pi * (
        coords[0][:, None] * wave_block[0][None, :]
        + coords[1][:, None] * wave_block[1][None, :]
        + coords[2][:, None] * wave_block[2][None, :]
    )
    return (jnp.cos(angles).astype(jnp.bfloat16), jnp.sin(angles).astype(jnp.bfloat16))


def responses(sums, wave_float, screening):
    norm_sq = jnp.sum(wave_float * wave_float, axis=0)
    kernel = jnp.exp(-norm_sq / ewald_width)[None, :] / (norm_sq[None, :] + screening[:, None])
    latent = screening.shape[0]
    return jnp.concatenate([kernel * sums[:latent], kernel * sums[latent:]], axis=0).astype(
        jnp.bfloat16
    )


def shards(
    features,
    frac,
    neighbours,
    nbr_mask,
    send_list,
    wavevectors,
    w_in,
    w_filter1,
    w_filter2,
    w_update1,
    w_update2,
    w_charge,
    screening,
    w_head,
    w_potential,
    w_energy,
):
    pos_send = jnp.take(frac, send_list, axis=1).reshape(3, HALO_SIDE, HALO_SIDE)
    pos_halo = with_halo(pos_send, (("gx", 1), ("yz", 2)), HALO_SIDE)
    pos_table = jnp.concatenate([frac, pos_halo.reshape(3, 9 * HALO_DEV)], axis=1)
    block_size = min(256, ATOMS_DEV)
    starts = jnp.arange(ATOMS_DEV // block_size, dtype=jnp.int32) * block_size
    inv_root = 1.0 / math.sqrt(K)
    state = features
    for layer_index in range(LAYERS):
        projected = jnp.dot(state, w_in[layer_index], preferred_element_type=jnp.float32).astype(
            jnp.bfloat16
        )
        send_rows = jnp.take(projected, send_list, axis=0).reshape(HALO_SIDE, HALO_SIDE, C)
        halo_rows = with_halo(send_rows, (("gx", 0), ("yz", 1)), HALO_SIDE)
        slot_table = jnp.concatenate([projected, halo_rows.reshape(9 * HALO_DEV, C)], axis=0)
        first_w = w_filter1[layer_index]
        second_w = w_filter2[layer_index]

        def edge_block(offset):
            slot_ids = lax.dynamic_slice_in_dim(neighbours, offset, block_size, 1)
            live_mask = lax.dynamic_slice_in_dim(nbr_mask, offset, block_size, 1)
            own_pos = lax.dynamic_slice_in_dim(frac, offset, block_size, 1)
            others = jnp.take(pos_table, slot_ids, axis=1)
            sines = jnp.sin(math.pi * (others - own_pos[:, None, :]))
            chord_sq = jnp.sum(sines * sines, axis=0)
            radial = radial_basis(chord_sq, NR)
            filter_hidden = jax.nn.silu(
                jnp.einsum("kbr,rc->kbc", radial, first_w, preferred_element_type=jnp.float32)
            ).astype(jnp.bfloat16)
            filters = jnp.einsum(
                "kbc,cd->kbd", filter_hidden, second_w, preferred_element_type=jnp.float32
            )
            sources = jnp.take(slot_table, slot_ids, axis=0)
            message = (
                filters * sources.astype(jnp.float32) * live_mask[..., None].astype(jnp.float32)
            )
            return (jnp.sum(message, axis=0) * inv_root).astype(jnp.bfloat16)

        aggregate = lax.map(edge_block, starts).reshape(ATOMS_DEV, C)
        update = jax.nn.silu(
            jnp.dot(aggregate, w_update1[layer_index], preferred_element_type=jnp.float32)
        ).astype(jnp.bfloat16)
        state = (
            state.astype(jnp.float32)
            + jnp.dot(update, w_update2[layer_index], preferred_element_type=jnp.float32)
        ).astype(jnp.bfloat16)
    charges = lax.dot_general(
        w_charge, state, (((0,), (1,)), ((), ())), preferred_element_type=jnp.float32
    ).astype(jnp.bfloat16)
    wave_all = lax.all_gather(wavevectors, ("gx", "yz"), axis=1, tiled=True).astype(jnp.float32)
    mode_block = min(256, MODES)
    mode_turns = MODES // mode_block
    mode_starts = jnp.arange(mode_turns, dtype=jnp.int32) * mode_block

    def factor_block(offset):
        wave_block = lax.dynamic_slice_in_dim(wave_all, offset, mode_block, 1)
        cos_part, sine_part = mode_phases(frac, wave_block)
        return jnp.concatenate(
            [
                jnp.dot(charges, cos_part, preferred_element_type=jnp.float32),
                jnp.dot(charges, sine_part, preferred_element_type=jnp.float32),
            ],
            axis=0,
        )

    stacked = lax.map(factor_block, mode_starts)
    partial_sums = stacked.transpose(1, 0, 2).reshape(2 * Q, MODES)
    total_sums = lax.psum(partial_sums, ("gx", "yz"))
    answer = responses(total_sums, wave_all, screening)
    contract = (((1,), (1,)), ((), ()))

    def potential_step(turn, running):
        offset = turn * mode_block
        wave_block = lax.dynamic_slice_in_dim(wave_all, offset, mode_block, 1)
        cos_part, sine_part = mode_phases(frac, wave_block)
        resp_block = lax.dynamic_slice_in_dim(answer, offset, mode_block, 1)
        return (
            running
            + lax.dot_general(
                resp_block[:Q], cos_part, contract, preferred_element_type=jnp.float32
            )
            + lax.dot_general(
                resp_block[Q:], sine_part, contract, preferred_element_type=jnp.float32
            )
        )

    field = lax.fori_loop(0, mode_turns, potential_step, jnp.zeros((Q, ATOMS_DEV), jnp.float32))
    atoms_total = ATOMS_DEV * lax.axis_size("gx") * lax.axis_size("yz")
    potentials = field * (4.0 / math.sqrt(atoms_total))
    potential_input = potentials.astype(jnp.bfloat16)
    summed = jnp.dot(state, w_head, preferred_element_type=jnp.float32) + lax.dot_general(
        potential_input, w_potential, (((0,), (0,)), ((), ())), preferred_element_type=jnp.float32
    )
    readout = jax.nn.silu(summed).astype(jnp.bfloat16)
    energies = jnp.dot(readout, w_energy, preferred_element_type=jnp.float32)
    return (state, potentials, energies)


def solution(mesh):
    return jax.shard_map(
        shards,
        mesh=mesh,
        in_specs=(
            P(("gx", "yz"), None),
            P(None, ("gx", "yz")),
            P(None, ("gx", "yz")),
            P(None, ("gx", "yz")),
            P(("gx", "yz")),
            P(None, ("gx", "yz")),
            P(),
            P(),
            P(),
            P(),
            P(),
            P(),
            P(),
            P(),
            P(),
            P(),
        ),
        out_specs=(P(("gx", "yz"), None), P(None, ("gx", "yz")), P(("gx", "yz"))),
        check_vma=False,
    )
```

profile of v0, /device:TPU:0, one launch (start us, length us, event | category | flops | bytes accessed | tf_op | source)
XLA Modules:
  0.0 833.6 jit_solution(184110952946579871)
XLA Ops:
  19.4 5.6 collective-permute-start.1
  27.3 3.8 collective-permute-start.3
  33.2 4.1 collective-permute-start.7
  37.8 4.2 collective-permute-done.6
  42.2 137.7 %while.48 = (s32[]{:T(128)}, bf16[2,256,128]{2,1,0:T(8,128)(2,1)S(1)}, s32[2]{0:T(128)}, s32[32,512]{1,0:T(8,128)S(1)}, f32[3,2816]{0,1:T(8,128)S(1)}, /*index=5...) while((s32[]{:T(128)}, ...), condition=%wide.region_3.7_spmd, body=%wide.region_0.6_spmd.sunk | while | flops 347578400 | bytes 7644607 | solution.py:117
  45.5 27.8 %gather_fusion.1 = f32[8192,3]{1,0:T(8,128)} fusion(f32[3,2816]{0,1:T(8,128)S(1)} %get-tuple-element.828, s32[8192]{0:T(1024)S(1)} %broadcast_clamp_fusion.4), kind=kCustom, calls=%fused_computation.1.clone.clone.1 | custom fusion | bytes 229376 | tf_op jit(solution)/shard_map/while/body/eval_jaxpr/jit(_take)/gather | solution.py:101
  76.8 29.4 %gather_fusion = bf16[8192,128]{1,0:T(8,128)(2,1)} fusion(bf16[2816,128]{1,0:T(8,128)(2,1)S(1)} %get-tuple-element.832, s32[8192]{0:T(1024)S(1)} %broadcast_clamp_fusion.4), kind=kCustom, calls=%fused_computation.2.clone.clone.1 | custom fusion | bytes 4227072 | tf_op jit(solution)/shard_map/while/body/eval_jaxpr/jit(_take)/gather | solution.py:111
  106.3 4.7 multiply_reduce_fusion.5
  114.3 27.8 %gather_fusion.1 = f32[8192,3]{1,0:T(8,128)} fusion(f32[3,2816]{0,1:T(8,128)S(1)} %get-tuple-element.828, s32[8192]{0:T(1024)S(1)} %broadcast_clamp_fusion.4), kind=kCustom, calls=%fused_computation.1.clone.clone.1 | custom fusion | bytes 229376 | tf_op jit(solution)/shard_map/while/body/eval_jaxpr/jit(_take)/gather | solution.py:101
  145.5 29.4 %gather_fusion = bf16[8192,128]{1,0:T(8,128)(2,1)} fusion(bf16[2816,128]{1,0:T(8,128)(2,1)S(1)} %get-tuple-element.832, s32[8192]{0:T(1024)S(1)} %broadcast_clamp_fusion.4), kind=kCustom, calls=%fused_computation.2.clone.clone.1 | custom fusion | bytes 4227072 | tf_op jit(solution)/shard_map/while/body/eval_jaxpr/jit(_take)/gather | solution.py:111
  175.1 4.7 multiply_reduce_fusion.5
  183.2 4.5 collective-permute-start.9
  190.5 3.8 collective-permute-start.11
  194.3 173.4 %all-gather = s32[128,32,3]{1,2,0:T(4,128)S(1)} all-gather(s32[1,32,3]{1,2,0:T(4,128)S(1)} %bitcast.264), channel_id=1, replica_groups=mesh['gx'=8,'yz'=16] {'gx','yz'}, dimensions={0}, use_global_device_ids=true | all-gather | bytes 49536 | tf_op jit(solution)/shard_map/all_gather | solution.py:128
  368.9 138.1 %while.49 = (s32[]{:T(128)}, bf16[2,256,128]{2,1,0:T(8,128)(2,1)S(1)}, s32[2]{0:T(128)}, s32[32,512]{1,0:T(8,128)S(1)}, f32[3,2816]{0,1:T(8,128)S(1)}, /*index=5...) while((s32[]{:T(128)}, ...), condition=%wide.region_7.11_spmd, body=%wide.region_4.0_spmd.sunk | while | flops 347578400 | bytes 7677403 | solution.py:117
  372.4 27.8 %gather_fusion.3 = f32[8192,3]{1,0:T(8,128)} fusion(f32[3,2816]{0,1:T(8,128)S(1)} %get-tuple-element.867, s32[8192]{0:T(1024)S(1)} %broadcast_clamp_fusion.5), kind=kCustom, calls=%fused_computation.4.clone.clone.1 | custom fusion | bytes 229376 | tf_op jit(solution)/shard_map/while/body/eval_jaxpr/jit(_take)/gather | solution.py:101
  403.6 29.4 %gather_fusion.2 = bf16[8192,128]{1,0:T(8,128)(2,1)} fusion(bf16[2816,128]{1,0:T(8,128)(2,1)S(1)} %get-tuple-element.871, s32[8192]{0:T(1024)S(1)} %broadcast_clamp_fusion.5), kind=kCustom, calls=%fused_computation.5.clone.clone.1 | custom fusion | bytes 4227072 | tf_op jit(solution)/shard_map/while/body/eval_jaxpr/jit(_take)/gather | solution.py:111
  433.2 4.7 multiply_reduce_fusion.6
  441.4 27.8 %gather_fusion.3 = f32[8192,3]{1,0:T(8,128)} fusion(f32[3,2816]{0,1:T(8,128)S(1)} %get-tuple-element.867, s32[8192]{0:T(1024)S(1)} %broadcast_clamp_fusion.5), kind=kCustom, calls=%fused_computation.4.clone.clone.1 | custom fusion | bytes 229376 | tf_op jit(solution)/shard_map/while/body/eval_jaxpr/jit(_take)/gather | solution.py:101
  472.7 29.4 %gather_fusion.2 = bf16[8192,128]{1,0:T(8,128)(2,1)} fusion(bf16[2816,128]{1,0:T(8,128)(2,1)S(1)} %get-tuple-element.871, s32[8192]{0:T(1024)S(1)} %broadcast_clamp_fusion.5), kind=kCustom, calls=%fused_computation.5.clone.clone.1 | custom fusion | bytes 4227072 | tf_op jit(solution)/shard_map/while/body/eval_jaxpr/jit(_take)/gather | solution.py:111
  502.2 4.7 multiply_reduce_fusion.6
  508.2 107.9 %while.50 = (s32[]{:T(128)}, f32[16,32,256]{2,1,0:T(8,128)S(1)}, f32[3,512]{1,0:T(4,128)S(1)}, s32[16]{0:T(128)S(1)}, f32[3,4096]{1,0:T(4,128)S(1)}, /*index=5*/...) while((s32[]{:T(128)}, f32[16,32,256]{2,1,0:T(8,128)S(1)}, ...), condition=%wide.region_10.14_spmd, body=%wide.region_9.13_spmd.sunk | while | flops 10231815 | bytes 168131 | solution.py:144
  617.2 139.6 %all-reduce.2.cloned.1.call-done = f32[32,4096]{1,0:T(8,128)} async-done(((f32[32,4096]{1,0:T(8,128)}), f32[32,4096]{1,0:T(8,128)}) %all-reduce.2.cloned.1.call-update) | async-done | bytes 524304 | tf_op jit(solution)/shard_map/psum | solution.py:146
  757.9 67.6 %while.51 = (s32[]{:T(128)}, f32[16,512]{1,0:T(8,128)S(1)}, bf16[32,4096]{1,0:T(8,128)(2,1)S(1)}, f32[3,512]{1,0:T(4,128)S(1)}, f32[3,4096]{1,0:T(4,128)S(1)}, /...) while((s32[]{:T(128)}, f32[16,512]{1,0:T(8,128)S(1)}, ...), condition=%wide.region_13.17_spmd.clone, body=%wide.region_12.16_spmd.clone.sunk | while | flops 10248202 | bytes 184553 | solution.py:165
  (318 shorter events, 192.3 us)
Async XLA Ops:
  7.2 818.7 %copy-start = (bf16[128,128]{1,0:T(8,128)(2,1)S(1)}, bf16[128,128]{1,0:T(8,128)(2,1)}, u32[]{:S(2)}) copy-start(bf16[128,128]{1,0:T(8,128)(2,1)} %param.43) | copy-start | bytes 98308
  7.2 749.5 %all-reduce.2.cloned.1.call-start = ((), (), s32[]{:S(2)}) async-start(), calls=%async_computation | async-start | bytes 1048576 | tf_op jit(solution)/shard_map/psum | solution.py:146
  10.7 22.4 %collective-permute-start.4 = (bf16[16,16,128]{2,1,0:T(8,128)(2,1)S(1)}, bf16[16,16,128]{2,1,0:T(8,128)(2,1)S(1)}, u32[]{:S(2)}, u32[]{:S(2)}) collective-permute-start(bf16[16,16,128]{2,1,0:T(8,128)(2,1)S(1)} %bitcast.226), channel_id=1, source_target_pairs={{0,16},{16,32},{32,48},{48,64},{64,80},{80,96},{96,112},{112,0},{1... | collective-permute-start | bytes 196616 | tf_op jit(solution)/shard_map/ppermute | solution.py:29
  13.9 19.2 %collective-permute-start.5 = (bf16[16,16,128]{2,1,0:T(8,128)(2,1)S(1)}, bf16[16,16,128]{2,1,0:T(8,128)(2,1)S(1)}, u32[]{:S(2)}, u32[]{:S(2)}) collective-permute-start(bf16[16,16,128]{2,1,0:T(8,128)(2,1)S(1)} %bitcast.227), channel_id=1, source_target_pairs={{16,0},{32,16},{48,32},{64,48},{80,64},{96,80},{112,96},{0,112},{1... | collective-permute-start | bytes 196616 | tf_op jit(solution)/shard_map/ppermute | solution.py:32
  19.4 7.8 collective-permute-start
  19.4 7.7 collective-permute-start.1
  27.3 5.4 collective-permute-start.2
  27.3 5.4 collective-permute-start.3
  33.1 8.8 %collective-permute-start.6 = (bf16[48,16,128]{2,1,0:T(8,128)(2,1)S(1)}, bf16[48,16,128]{2,1,0:T(8,128)(2,1)S(1)}, u32[]{:S(2)}, u32[]{:S(2)}) collective-permute-start(bf16[48,16,128]{2,1,0:T(8,128)(2,1)S(1)} %pad_maximum_fusion.5), channel_id=1, source_target_pairs={{0,1},{1,2},{2,3},{3,4},{4,5},{5,6},{6,7},{7,8},{8,9},{9,10},{10,1... | collective-permute-start | bytes 589832 | tf_op jit(solution)/shard_map/ppermute | solution.py:29
  33.2 8.8 %collective-permute-start.7 = (bf16[48,16,128]{2,1,0:T(8,128)(2,1)S(1)}, bf16[48,16,128]{2,1,0:T(8,128)(2,1)S(1)}, u32[]{:S(2)}, u32[]{:S(2)}) collective-permute-start(bf16[48,16,128]{2,1,0:T(8,128)(2,1)S(1)} %pad_maximum_fusion.5), channel_id=1, source_target_pairs={{1,0},{2,1},{3,2},{4,3},{5,4},{6,5},{7,6},{8,7},{9,8},{10,9},{11,1... | collective-permute-start | bytes 589832 | tf_op jit(solution)/shard_map/ppermute | solution.py:32
  42.1 137.7 %copy-start.6 = (bf16[512,128]{1,0:T(8,128)(2,1)S(1)}, bf16[512,128]{1,0:T(8,128)(2,1)}, u32[]{:S(2)}) copy-start(bf16[512,128]{1,0:T(8,128)(2,1)} %param.30) | copy-start | bytes 393220
  42.1 137.7 %copy-start.15 = (bf16[2,128,128]{2,1,0:T(8,128)(2,1)S(1)}, bf16[2,128,128]{2,1,0:T(8,128)(2,1)}, u32[]{:S(2)}) copy-start(bf16[2,128,128]{2,1,0:T(8,128)(2,1)} %param.40) | copy-start | bytes 196612
  42.1 137.7 %copy-start.17 = (bf16[2,128,128]{2,1,0:T(8,128)(2,1)S(1)}, bf16[2,128,128]{2,1,0:T(8,128)(2,1)}, u32[]{:S(2)}) copy-start(bf16[2,128,128]{2,1,0:T(8,128)(2,1)} %param.39) | copy-start | bytes 196612
  42.1 138.7 %copy-start.9 = (bf16[2,128,128]{2,1,0:T(8,128)(2,1)S(1)}, bf16[2,128,128]{2,1,0:T(8,128)(2,1)}, u32[]{:S(2)}) copy-start(bf16[2,128,128]{2,1,0:T(8,128)(2,1)} %param.36) | copy-start | bytes 196612
  182.0 8.3 collective-permute-start.8
  183.2 7.1 collective-permute-start.9
  190.4 178.3 %collective-permute-start.10 = (bf16[48,16,128]{2,1,0:T(8,128)(2,1)S(1)}, bf16[48,16,128]{2,1,0:T(8,128)(2,1)S(1)}, u32[]{:S(2)}, u32[]{:S(2)}) collective-permute-start(bf16[48,16,128]{2,1,0:T(8,128)(2,1)S(1)} %pad_maximum_fusion.6), channel_id=1, source_target_pairs={{0,1},{1,2},{2,3},{3,4},{4,5},{5,6},{6,7},{7,8},{8,9},{9,10},{10,1... | collective-permute-start | bytes 589832 | tf_op jit(solution)/shard_map/ppermute | solution.py:29
  190.5 178.2 %collective-permute-start.11 = (bf16[48,16,128]{2,1,0:T(8,128)(2,1)S(1)}, bf16[48,16,128]{2,1,0:T(8,128)(2,1)S(1)}, u32[]{:S(2)}, u32[]{:S(2)}) collective-permute-start(bf16[48,16,128]{2,1,0:T(8,128)(2,1)S(1)} %pad_maximum_fusion.6), channel_id=1, source_target_pairs={{1,0},{2,1},{3,2},{4,3},{5,4},{6,5},{7,6},{8,7},{9,8},{10,9},{11,1... | collective-permute-start | bytes 589832 | tf_op jit(solution)/shard_map/ppermute | solution.py:32
  368.8 138.2 %copy-start.8 = (bf16[512,128]{1,0:T(8,128)(2,1)S(1)}, bf16[512,128]{1,0:T(8,128)(2,1)}, u32[]{:S(2)}) copy-start(bf16[512,128]{1,0:T(8,128)(2,1)} %copy-done.7) | copy-start | bytes 393220
  368.8 138.1 %copy-start.16 = (bf16[2,128,128]{2,1,0:T(8,128)(2,1)S(1)}, bf16[2,128,128]{2,1,0:T(8,128)(2,1)}, u32[]{:S(2)}) copy-start(bf16[2,128,128]{2,1,0:T(8,128)(2,1)} %param.40) | copy-start | bytes 196612
  368.8 139.2 %copy-start.12 = (bf16[128,16]{0,1:T(8,128)(2,1)S(1)}, bf16[128,16]{0,1:T(8,128)(2,1)}, u32[]{:S(2)}) copy-start(bf16[128,16]{0,1:T(8,128)(2,1)} %param.41) | copy-start | bytes 12292
  368.8 139.4 %copy-start.19 = (s32[16]{0:T(128)S(1)}, s32[16]{0:T(128)}, u32[]{:S(2)}) copy-start(s32[16]{0:T(128)} %iota_multiply_fusion.2) | copy-start | bytes 196
  508.1 317.7 %copy-start.5 = (bf16[512,128]{1,0:T(8,128)(2,1)}, bf16[512,128]{1,0:T(8,128)(2,1)S(1)}, u32[]{:S(2)}) copy-start(bf16[512,128]{1,0:T(8,128)(2,1)S(1)} %fusion.93) | copy-start | bytes 393220
  508.2 248.5 %copy-start.14 = (f32[16]{0:T(128)S(1)}, f32[16]{0:T(128)}, u32[]{:S(2)}) copy-start(f32[16]{0:T(128)} %param.42) | copy-start | bytes 196
  (10 other events, 250.7 us)
Sparse Core Ops, SparseCore 0:
  617.2 139.4 all-reduce.1
where the time goes:
time: 836 us; the launch traced here: 834 us
  local copies, waits for them, and re-layouts  267 us (32%)
  blocking collectives  173 us (21%)
  matrix products  154 us (18%)
  waiting for transfers between devices  147 us (18%)
  loops' own time  39.7 us (5%)
  starting transfers between devices  30.1 us (4%)
  between operations  14.6 us (2%)
    all_gather x1, blocking collectives, shards(): lax.all_gather(wavevectors, ('gx', 'yz'), axis=1, tiled=True)  173 us
    psum x1, waiting for transfers between devices, shards(): total_sums = lax.psum(partial_sums, ('gx', 'yz'))  140 us
    gather x8, local copies, waits for them, and re-layouts, edge_block(): others = jnp.take(pos_table, slot_ids, axis=1)  123 us
    gather x4, local copies, waits for them, and re-layouts, edge_block(): sources = jnp.take(slot_table, slot_ids, axis=0)  118 us
    dot_general x16, matrix products, potential_step(): lax.dot_general(resp_block[Q:], sine_part, contract, preferred_element_ty...  33.2 us
    dot_general x16, matrix products, factor_block(): jnp.dot(charges, sine_part, preferred_element_type=jnp.float32)  33.1 us
    dot_general x16, matrix products, potential_step(): lax.dot_general(resp_block[:Q], cos_part, contract, preferred_element_typ...  32.8 us
    dot_general x16, matrix products, factor_block(): jnp.dot(charges, cos_part, preferred_element_type=jnp.float32)  32.1 us
  transfers between devices with their start and end apart: 13, of which 4 were waited for; matrix products, arithmetic and copies ran while one was open for 1% of the time, Pallas kernels for 0%

commit v1 on v0

v1 whole, which is shorter than its diff:
```python
import functools
import math

import jax
import jax.numpy as jnp
from jax import lax
from jax.experimental import pallas as pl
from jax.experimental.pallas import tpu as pltpu
from jax.sharding import PartitionSpec as P

C = 128
NR = 32
Q = 16
K = 32
SIDE = 16
T = 512
H = 256
PACK = H + 32
SLOTS = T + 9 * H
ZERO = SLOTS
PIECES = SLOTS // 128
KX = 7
YZ = 13
BETA = 176
ROWS = KX * Q
SUM_ROWS = ROWS + 16
SUM_LANES = 384
f32, bf16, i32 = jnp.float32, jnp.bfloat16, jnp.int32


def rows_of(shape, dim):
    return lax.broadcasted_iota(i32, shape, dim)


def dot(a, b, dims=((1,), (0,))):
    return lax.dot_general(a, b, (dims, ((), ())), preferred_element_type=f32)


def silu(v):
    half = 0.5 * v
    return half + half * jnp.tanh(half)


def sin_pi(x):
    y = x * x
    total = jnp.full_like(x, math.pi**13 / math.factorial(13))
    for order in (11, 9, 7, 5, 3, 1):
        sign = -1.0 if order % 4 == 3 else 1.0
        total = total * y + sign * math.pi**order / math.factorial(order)
    return total * x


def pick8(table, index_of):
    sub = rows_of((8, C), 0)
    picked = table[pl.ds(index_of(0), 8, stride=0), :]
    for j in range(1, 8):
        picked = jnp.where(sub == j, table[pl.ds(index_of(j), 8, stride=0), :], picked)
    return picked


def pick_send_rows(table, send, out):
    def group(g, carry):
        base = g * 16
        low = pick8(table, lambda j: send[base + j])
        high = pick8(table, lambda j: send[base + 8 + j])
        out[pl.ds(pl.multiple_of(base, 16), 16), :] = jnp.concatenate([low, high], axis=0).astype(bf16)
        return carry

    lax.fori_loop(0, H // 16, group, 0)


def first_kernel(send, send_lanes, features, frac, w_in, proj_out, out, table, parts):
    projected = dot(features[...], w_in[0]).astype(bf16)
    proj_out[...] = projected
    table[...] = projected.astype(f32)
    pick_send_rows(table, send, out)
    parts[...] = jnp.zeros_like(parts)
    for half in range(2):
        index = jnp.broadcast_to(send_lanes[half : half + 1, :], (8, 128))
        low, high = index & 127, index >> 7
        for c in range(3):
            value = jnp.zeros((8, 128), f32)
            for p in range(T // 128):
                source = jnp.broadcast_to(frac[c : c + 1, p * 128 : (p + 1) * 128], (8, 128))
                value = jnp.where(high == p, jnp.take_along_axis(source, low, axis=1), value)
            value = value[0:1]
            for part in range(3):
                rounded = value.astype(bf16).astype(f32)
                row = part * 8 + half * 4 + c
                parts[row : row + 1, :] = rounded
                value = value - rounded
    out[H:PACK, :] = parts[...].astype(bf16)


def prepare_kernel(neighbours, mask, frac, waves, slots_out, phase_out, axis_out, digits_out, plane):
    u = neighbours[...] - T
    row = (u * 43691) >> 21
    col = u - row * 48
    block = (col >> 4) * 3 + (row >> 4)
    moved = T + block * H + (row & 15) * SIDE + (col & 15)
    slots = jnp.where(mask[...] != 0, jnp.where(u < 0, u + T, moved), ZERO)
    for b in range(T // 128):
        slots_out[b * K : (b + 1) * K, :] = slots[:, b * 128 : (b + 1) * 128]

    def turn(c):
        harmonics = []
        for n in range(KX):
            x = frac[c : c + 1, :] * float(n)
            x = x - jnp.floor(x + 0.5)
            s = sin_pi(jnp.clip(2.0 * x - jnp.floor(2.0 * x + 0.5), -0.5, 0.5))
            odd = (jnp.floor(2.0 * x + 0.5).astype(i32) & 1) != 0
            sine = jnp.where(odd, -s, s)
            y = 2.0 * x + 0.5
            t = y - jnp.floor(y + 0.5)
            s2 = sin_pi(jnp.clip(t, -0.5, 0.5))
            odd2 = (jnp.floor(y + 0.5).astype(i32) & 1) != 0
            cosine = jnp.where(odd2, -s2, s2)
            harmonics.append((cosine, sine))
        return harmonics

    hx, hy, hz = turn(0), turn(1), turn(2)
    axis_out[...] = jnp.zeros_like(axis_out)
    for n in range(KX):
        axis_out[n : n + 1, :] = hx[n][0]
        axis_out[8 + n : 9 + n, :] = hx[n][1]

    def signed(h, k):
        c, s = h[abs(k)]
        return (c, s) if k >= 0 else (c, -s)

    zc = jnp.concatenate([signed(hz, k)[0] for k in range(-6, 7)], axis=0)
    zs = jnp.concatenate([signed(hz, k)[1] for k in range(-6, 7)], axis=0)
    plane[...] = jnp.zeros_like(plane)
    for n in range(YZ):
        yc, ys = signed(hy, n - 6)
        c = yc * zc - ys * zs
        s = ys * zc + yc * zs
        plane[0, n * YZ : (n + 1) * YZ, :] = c
        plane[1, n * YZ : (n + 1) * YZ, :] = s
    phase_out[:BETA, :T] = plane[0].astype(bf16)
    phase_out[:BETA, T:] = (-plane[1]).astype(bf16)
    phase_out[BETA:, :T] = plane[1].astype(bf16)
    phase_out[BETA:, T:] = plane[0].astype(bf16)

    modes = waves.shape[1]
    flip = jnp.where(waves[0:1, :] < 0, -1, 1)
    kx = waves[0:1, :] * flip
    beta = (waves[1:2, :] * flip + 6) * YZ + waves[2:3, :] * flip + 6
    hot_x = (rows_of((8, modes), 0) == kx).astype(f32).astype(bf16)
    r = rows_of((SUM_LANES, modes), 0)
    r = jnp.where(r >= BETA, r - BETA, r)
    hot_b = (r == beta).astype(f32).astype(bf16)
    count = dot(hot_x, hot_b, ((1,), (1,))).astype(i32)
    thirds = [count]
    for _ in range(3):
        thirds.append((thirds[-1] * 171) >> 9)
    digit = [a - 3 * b for a, b in zip(thirds[:3], thirds[1:])] + [thirds[3]]
    lane = rows_of((8, SUM_LANES), 1)
    first = lane < BETA
    keep = lane < 2 * BETA
    low = jnp.where(first, digit[0], digit[2])
    high = jnp.where(first, digit[1], digit[3])
    digits_out[0:8, :] = jnp.where(keep, low, 0).astype(f32)
    digits_out[8:16, :] = jnp.where(keep, high, 0).astype(f32)


def fill_table(table, projected, rows_in, stride):
    table[0:T, :] = projected[...].astype(f32)
    for by in range(3):
        for bx in range(3):
            at = T + (by * 3 + bx) * H
            table[at : at + H, :] = rows_in[by][bx * stride : bx * stride + H, :].astype(f32)
    table[ZERO : ZERO + 8, :] = jnp.zeros((8, C), f32)


def fill_filter_weights(w1, w2, layer, wide1, wide2):
    wide1[...] = jnp.zeros_like(wide1)
    wide2[...] = jnp.zeros_like(wide2)
    for j in range(4):
        wide1[j * NR : (j + 1) * NR, j * C : (j + 1) * C] = w1[layer]
    for j in range(2):
        wide2[j * C : (j + 1) * C, j * C : (j + 1) * C] = w2[layer]


def filters_of(chord_rows, wide1, wide2):
    inv_width = 31.0 / 3.0
    centre = rows_of((NR, 128), 0).astype(f32)
    radial = []
    for chord in chord_rows:
        scaled = chord * inv_width - centre
        radial.append(jnp.exp(-0.5 * scaled * scaled))
    radial = jnp.concatenate(radial, axis=0).astype(bf16)
    hidden = silu(dot(radial, wide1[...], ((0,), (0,)))).astype(bf16)
    return (dot(hidden[:, : 2 * C], wide2[...]), dot(hidden[:, 2 * C :], wide2[...]))


def update_tail(total, state, w_update1, w_update2, layer):
    aggregate = (total[...] * (1.0 / math.sqrt(K))).astype(bf16)
    update = silu(dot(aggregate, w_update1[layer])).astype(bf16)
    return (state[...].astype(f32) + dot(update, w_update2[layer])).astype(bf16)


def chords(slots, frac, rows_in, chord, places):
    for c in range(3):
        for p in range(T // 128):
            places[c * 24 + p : c * 24 + p + 1, :] = frac[c : c + 1, p * 128 : (p + 1) * 128]
    for by in range(3):
        for bx in range(3):
            part = rows_in[by][bx * PACK + H : (bx + 1) * PACK, :].astype(f32)
            value = part[0:8] + part[8:16] + part[16:24]
            for half in range(2):
                p = T // 128 + (by * 3 + bx) * 2 + half
                for c in range(3):
                    at = c * 24 + p
                    places[at : at + 1, :] = value[half * 4 + c : half * 4 + c + 1]

    def lane_block(b, carry):
        lanes = pl.ds(pl.multiple_of(b * 128, 128), 128)
        for g in range(K // 8):
            index = slots[pl.ds(pl.multiple_of(b * K + g * 8, 8), 8), :]
            low, high = index & 127, index >> 7
            total = jnp.zeros((8, 128), f32)
            value = [jnp.zeros((8, 128), f32) for _ in range(3)]
            for p in range(PIECES):
                here = high == p
                for c in range(3):
                    source = places[pl.ds(c * 24 + p, 8, stride=0), :]
                    value[c] = jnp.where(here, jnp.take_along_axis(source, low, axis=1), value[c])
            for c in range(3):
                apart = value[c] - frac[c : c + 1, lanes]
                apart = apart - jnp.floor(apart + 0.5)
                sine = sin_pi(apart)
                total = total + sine * sine
            chord[pl.ds(pl.multiple_of(b * K + g * 8, 8), 8), :] = total
        return carry

    lax.fori_loop(0, T // 128, lane_block, 0)


def add_messages(table, slots, filters, total, block, group):
    first = block * (K * 128) + group * 512
    for g in range(16):
        start = block * 128 + g * 8
        at = pl.ds(pl.multiple_of(start, 8), 8)
        acc = total[at, :]
        for j in range(4):
            source = pick8(table, lambda s: slots[first + (j * 128 + g * 8 + s)])
            acc = acc + source * filters[g * 8 : g * 8 + 8, j * C : (j + 1) * C]
        total[at, :] = acc


def layer_kernel(
    slots_s, send, slots, frac, x_low, x_own, x_high, projected, state,
    w1, w2, w_update1, w_update2, w_in,
    state_out, proj_out, send_out, chord_out,
    table, places, wide1, wide2, ping, pong, total, proj_table,
):
    rows_in = (x_low, x_own, x_high)
    fill_table(table, projected, rows_in, PACK)
    fill_filter_weights(w1, w2, 0, wide1, wide2)
    chords(slots, frac, rows_in, chord_out, places)
    total[...] = jnp.zeros_like(total)

    def make(step, buffer):
        block, group = step // 8, step % 8
        rows = [chord_out[pl.ds(block * K + group * 4 + j, NR, stride=0), :] for j in range(4)]
        a, b = filters_of(rows, wide1, wide2)
        buffer[:, : 2 * C] = a
        buffer[:, 2 * C :] = b

    def use(step, buffer):
        add_messages(table, slots_s, buffer, total, step // 8, step % 8)

    make(0, ping)

    def pair(i, carry):
        make(2 * i + 1, pong)
        use(2 * i, ping)
        make(jnp.minimum(2 * i + 2, 31), ping)
        use(2 * i + 1, pong)
        return carry

    lax.fori_loop(0, 16, pair, 0)
    new_state = update_tail(total, state, w_update1, w_update2, 0)
    state_out[...] = new_state
    projected1 = dot(new_state, w_in[1]).astype(bf16)
    proj_out[...] = projected1
    proj_table[...] = projected1.astype(f32)
    pick_send_rows(proj_table, send, send_out)


def filter_kernel(chord, w1, w2, out, wide1, wide2):
    @pl.when(pl.program_id(0) == 0)
    def _():
        fill_filter_weights(w1, w2, 1, wide1, wide2)

    first = pl.program_id(0) * K

    def group(g, carry):
        rows = [chord[pl.ds(first + g * 4 + j, NR, stride=0), :] for j in range(4)]
        a, b = filters_of(rows, wide1, wide2)
        out[g, :, : 2 * C] = a.astype(bf16)
        out[g, :, 2 * C :] = b.astype(bf16)
        return carry

    lax.fori_loop(0, 8, group, 0)


def last_layer_kernel(
    slots_s, filters, x_low, x_own, x_high, projected, state,
    w_update1, w_update2, w_charge, phase, axis, digits,
    state_out, sums_out,
    table, total, left,
):
    block = pl.program_id(0)

    @pl.when(block == 0)
    def _():
        fill_table(table, projected, (x_low, x_own, x_high), H)
        total[...] = jnp.zeros_like(total)

    def group(g, carry):
        add_messages(table, slots_s, filters.at[g], total, block, g)
        return carry

    lax.fori_loop(0, 8, group, 0)

    @pl.when(block == T // 128 - 1)
    def _():
        new_state = update_tail(total, state, w_update1, w_update2, 1)
        state_out[...] = new_state
        charges = dot(w_charge[...], new_state, ((0,), (1,))).astype(bf16).astype(f32)
        for n in range(KX):
            left[n * Q : (n + 1) * Q, :T] = (charges * axis[n : n + 1, :]).astype(bf16)
            left[n * Q : (n + 1) * Q, T:] = (charges * axis[8 + n : 9 + n, :]).astype(bf16)
        sums_out[...] = jnp.zeros_like(sums_out)
        sums_out[:ROWS, : 2 * BETA] = dot(left[...], phase[...], ((1,), (1,))).astype(bf16)
        sums_out[ROWS:, :] = digits[...].astype(bf16)


def field_kernel(
    sums, phase, axis, screening, state, w_head, w_potential, w_energy,
    potentials_out, energies_out, response,
):
    lane = rows_of((1, SUM_LANES), 1)
    beta = jnp.where(lane >= BETA, lane - BETA, lane)
    y = (beta * 79) >> 10
    ky = y - 6
    kz = beta - y * YZ - 6
    plane_sq = (ky * ky + kz * kz).astype(f32)
    digits = sums[ROWS:, :].astype(f32)
    packed = digits[0:8] + 3.0 * digits[8:16]
    ahead = pltpu.roll(packed, SUM_LANES - BETA, 1)
    behind = pltpu.roll(packed, BETA, 1)
    lane8 = rows_of((8, SUM_LANES), 1)
    count = jnp.where(lane8 < BETA, packed + 9.0 * ahead, behind + 9.0 * packed)
    square = rows_of((Q, Q), 0) == rows_of((Q, Q), 1)
    screen = jnp.sum(jnp.where(square, jnp.broadcast_to(screening[...], (Q, Q)), 0.0), axis=1, keepdims=True)
    for n in range(KX):
        norm_sq = plane_sq + float(n * n)
        kernel = jnp.exp(norm_sq * (-1.0 / 64.0)) * count[n : n + 1, :] / (norm_sq + screen)
        value = kernel * sums[n * Q : (n + 1) * Q, :].astype(f32)
        response[n * Q : (n + 1) * Q, :] = value[:, : 2 * BETA].astype(bf16)
    field = dot(response[...], phase[...])
    total = jnp.zeros((Q, T), f32)
    for n in range(KX):
        part = field[n * Q : (n + 1) * Q]
        total = total + part[:, :T] * axis[n : n + 1, :] + part[:, T:] * axis[8 + n : 9 + n, :]
    potentials = total * (4.0 / 256.0)
    potentials_out[...] = potentials
    summed = dot(state[...], w_head[...]) + dot(potentials.astype(bf16), w_potential[...], ((0,), (0,)))
    readout = silu(summed).astype(bf16)
    energies_out[...] = dot(w_energy[...], readout, ((1,), (1,)))


VMEM = pl.BlockSpec(memory_space=pltpu.VMEM)
SMEM = pl.BlockSpec(memory_space=pltpu.SMEM)


def shape(*dims, dtype=f32):
    return jax.ShapeDtypeStruct(dims, dtype)


def call(kernel, ins, outs, scratch, flops, moved):
    return pl.pallas_call(
        kernel,
        out_shape=outs,
        in_specs=ins,
        out_specs=jax.tree.map(lambda _: VMEM, outs),
        scratch_shapes=scratch,
        cost_estimate=pl.CostEstimate(flops=flops, bytes_accessed=moved, transcendentals=0),
    )


def halo(block):
    for axis in ("gx", "yz"):
        count = lax.axis_size(axis)
        forward = [(i, (i + 1) % count) for i in range(count)]
        backward = [(target, source) for source, target in forward]
        low = lax.ppermute(block, axis, forward)
        high = lax.ppermute(block, axis, backward)
        if axis == "gx":
            block = jnp.concatenate([low, block, high], axis=0)
    return low, block, high


STAGES = (("yz", (1, 2, 3)), ("yz", (4, 8, 12)), ("gx", (1, 2, 3)), ("gx", (4,)))


def sum_everywhere(part):
    for axis, offsets in STAGES:
        count = lax.axis_size(axis)
        taken = [lax.ppermute(part, axis, [(i, i ^ o) for i in range(count)]) for o in offsets]
        total = part.astype(f32)
        for one in taken:
            total = total + one.astype(f32)
        part = total.astype(bf16)
    return part


def shards(
    features, frac, neighbours, nbr_mask, send_list, wavevectors, w_in, w_filter1, w_filter2,
    w_update1, w_update2, w_charge, screening, w_head, w_potential, w_energy,
):
    projected, sent = call(
        first_kernel, [SMEM, VMEM, VMEM, VMEM, VMEM],
        (shape(T, C, dtype=bf16), shape(PACK, C, dtype=bf16)),
        [pltpu.VMEM((T, C), f32), pltpu.VMEM((32, 128), f32)], 20_000_000, 300_000,
    )(send_list, send_list.reshape(2, 128), features, frac, w_in)
    slots, phase, axis, digits = call(
        prepare_kernel, [VMEM] * 4,
        (shape(4 * K, 128, dtype=i32), shape(2 * BETA, 2 * T, dtype=bf16), shape(16, T), shape(16, SUM_LANES)),
        [pltpu.VMEM((2, BETA, T), f32)], 2_000_000_000, 4_000_000,
    )(neighbours, nbr_mask, frac, wavevectors)
    x_low, x_own, x_high = halo(sent)
    state, projected, sent, chord = call(
        layer_kernel, [SMEM, SMEM] + [VMEM] * 12,
        (shape(T, C, dtype=bf16), shape(T, C, dtype=bf16), shape(H, C, dtype=bf16), shape(4 * K, 128)),
        [
            pltpu.VMEM((SLOTS + 8, C), f32), pltpu.VMEM((72, 128), f32),
            pltpu.VMEM((4 * NR, 4 * C), bf16), pltpu.VMEM((2 * C, 2 * C), bf16),
            pltpu.VMEM((128, 4 * C), f32), pltpu.VMEM((128, 4 * C), f32),
            pltpu.VMEM((T, C), f32), pltpu.VMEM((T, C), f32),
        ], 4_000_000_000, 4_000_000,
    )(
        slots.reshape(-1), send_list, slots, frac, x_low, x_own, x_high, projected, features,
        w_filter1, w_filter2, w_update1, w_update2, w_in,
    )
    x_low, x_own, x_high = halo(sent)
    whole = lambda a: pl.BlockSpec(a.shape, lambda i: (0,) * a.ndim)
    block = pl.BlockSpec((8, 128, 4 * C), lambda i: (i, 0, 0))
    filters = pl.pallas_call(
        filter_kernel, grid=(T // 128,),
        out_shape=shape(32, 128, 4 * C, dtype=bf16),
        in_specs=[whole(chord), whole(w_filter1), whole(w_filter2)], out_specs=block,
        scratch_shapes=[pltpu.VMEM((4 * NR, 4 * C), bf16), pltpu.VMEM((2 * C, 2 * C), bf16)],
        cost_estimate=pl.CostEstimate(flops=4_000_000_000, bytes_accessed=8_000_000, transcendentals=0),
    )(chord, w_filter1, w_filter2)
    rest = (x_low, x_own, x_high, projected, state, w_update1, w_update2, w_charge, phase, axis, digits)
    embeddings, sums = pl.pallas_call(
        last_layer_kernel, grid=(T // 128,),
        out_shape=(shape(T, C, dtype=bf16), shape(SUM_ROWS, SUM_LANES, dtype=bf16)),
        in_specs=[SMEM, block] + [whole(a) for a in rest],
        out_specs=(pl.BlockSpec((T, C), lambda i: (0, 0)), pl.BlockSpec((SUM_ROWS, SUM_LANES), lambda i: (0, 0))),
        scratch_shapes=[pltpu.VMEM((SLOTS + 8, C), f32), pltpu.VMEM((T, C), f32), pltpu.VMEM((ROWS, 2 * T), bf16)],
        cost_estimate=pl.CostEstimate(flops=1_000_000_000, bytes_accessed=8_000_000, transcendentals=0),
    )(slots.reshape(-1), filters, *rest)
    sums = sum_everywhere(sums)
    potentials, energies = call(
        field_kernel, [VMEM] * 8, (shape(Q, T), shape(1, T)),
        [pltpu.VMEM((ROWS, 2 * BETA), bf16)], 100_000_000, 2_000_000,
    )(
        sums, phase, axis, screening.reshape(1, Q), embeddings, w_head, w_potential,
        w_energy.reshape(1, C),
    )
    return embeddings, potentials, energies.reshape(T)


def solution(mesh):
    atoms = ("gx", "yz")
    return jax.shard_map(
        shards,
        mesh=mesh,
        in_specs=(P(atoms, None), P(None, atoms), P(None, atoms), P(None, atoms), P(atoms), P(None, atoms))
        + (P(),) * 10,
        out_specs=(P(atoms, None), P(None, atoms), P(atoms)),
        check_vma=False,
    )
```

time: 836 us -> 125 us (0.15)
  local copies, waits for them, and re-layouts: 267 us -> 3.96 us
  blocking collectives: 173 us -> 0 us
  matrix products: 154 us -> 0 us
  waiting for transfers between devices: 147 us -> 28.2 us
  Pallas kernels: 0 us -> 60.5 us
  loops' own time: 39.7 us -> 0 us
  between operations: 14.6 us -> 0.73 us
    gather x16 -> x0, local copies, waits for them, and re-layouts: 243 us -> none  [the longest x8 123 us: edge_block(): others = jnp.take(pos_table, slot_ids, axis=1)]
    all_gather x1 -> x0, blocking collectives: 173 us -> none  [shards(): lax.all_gather(wavevectors, ('gx', 'yz'), axis=1, tiled=True)]
    dot_general x75 -> x0, matrix products: 154 us -> none  [the longest x16 33.2 us: potential_step(): lax.dot_general(resp_block[Q:], sine_part, contract, preferred_element_ty...]
    psum x1 -> x0, waiting for transfers between devices: 140 us -> none  [shards(): total_sums = lax.psum(partial_sums, ('gx', 'yz'))]
    pallas_call x0 -> x6, Pallas kernels: none -> 60.5 us  [the longest x1 23 us: shards(): call(layer_kernel, [SMEM, SMEM] + [VMEM] * 12, (shape(T, C, dtype=bf16),...]
    another operation x4 -> x0, loops' own time: 39.7 us -> none  [the longest x1 31.2 us: shards(): stacked = lax.map(factor_block, mode_starts)]
    ppermute x12 -> x18, waiting for transfers between devices: 7.71 us -> 28.2 us  [the longest x10 17.3 us: sum_everywhere(): lax.ppermute(part, axis, [(i, i ^ o) for i in range(count)])]
    dynamic_slice x24 -> x0, local copies, waits for them, and re-layouts: 15.4 us -> none  [the longest x16 9.97 us: shards(): stacked = lax.map(factor_block, mode_starts)]
  transfers between devices with their start and end apart: 13 -> 18, of which waited for: 4 -> 13; matrix products, arithmetic and copies ran while one was open for 1% -> 2% of each run, Pallas kernels for 0% -> 13%
where the time goes in v1:
time: 125 us
  Pallas kernels  60.5 us (48%)
  starting transfers between devices  29.4 us (24%)
  waiting for transfers between devices  28.2 us (23%)
  local copies, waits for them, and re-layouts  3.96 us (3%)
  other arithmetic  1.72 us (1%)
    pallas_call x1, Pallas kernels, shards(): call(layer_kernel, [SMEM, SMEM] + [VMEM] * 12, (shape(T, C, dtype=bf16),...  23 us
    ppermute x10, waiting for transfers between devices, sum_everywhere(): lax.ppermute(part, axis, [(i, i ^ o) for i in range(count)])  17.3 us
    pallas_call x1, Pallas kernels, shards(): pl.pallas_call(last_layer_kernel, grid=(T // 128,), out_shape=(shape(T, C...  16.9 us
    ppermute x10, starting transfers between devices, sum_everywhere(): lax.ppermute(part, axis, [(i, i ^ o) for i in range(count)])  14.9 us
    pallas_call x1, Pallas kernels, shards(): pl.pallas_call(filter_kernel, grid=(T // 128,), out_shape=shape(32, 128,...  13.7 us
    ppermute x4, waiting for transfers between devices, halo(): low = lax.ppermute(block, axis, forward)  7.67 us
    ppermute x4, starting transfers between devices, halo(): high = lax.ppermute(block, axis, backward)  7.52 us
    ppermute x4, starting transfers between devices, halo(): low = lax.ppermute(block, axis, forward)  7.02 us
  transfers between devices with their start and end apart: 18, of which 13 were waited for; matrix products, arithmetic and copies ran while one was open for 2% of the time, Pallas kernels for 13%

profile of v1, /device:TPU:0, one launch (start us, length us, event | category | flops | bytes accessed | tf_op | source)
XLA Modules:
  0.0 124.6 jit_solution(17720113917885107064)
XLA Ops:
  0.6 2.2 %shard_map.176 = (bf16[512,128]{1,0:T(8,128)(2,1)}, bf16[288,128]{1,0:T(8,128)(2,1)}) custom-call(s32[256]{0:T(256)} %send.3, s32[2,128]{1,0:T(2,128)} %bitcast.7, bf16[512,128]{1,0:T(8,128)(2,1)} %state.1, f32[3,512]{1,0:T(4,128)} %frac.5, bf16[2,128,128]{2,1,0:T(8,128)(2,1)} %w_in.3), custom_call_target="tpu_custom_call" | custom-call | flops 20000000 | bytes 300000 | tf_op jit(solution)/shard_map/pallas_call | solution.py:425
  2.8 3.1 %collective-permute-start = (bf16[288,128]{1,0:T(8,128)(2,1)}, bf16[288,128]{1,0:T(8,128)(2,1)S(1)}, u32[]{:S(2)}, u32[]{:S(2)}) collective-permute-start(bf16[288,128]{1,0:T(8,128)(2,1)} %get-tuple-element.18), channel_id=1, source_target_pairs={{0,16},{16,32},{32,48},{48,64},{64,80},{80,96},{96,112},{112,0},{1... | collective-permute-start | bytes 221192 | tf_op jit(solution)/shard_map/ppermute | solution.py:400
  5.9 3.5 %collective-permute-start.1 = (bf16[288,128]{1,0:T(8,128)(2,1)}, bf16[288,128]{1,0:T(8,128)(2,1)S(1)}, u32[]{:S(2)}, u32[]{:S(2)}) collective-permute-start(bf16[288,128]{1,0:T(8,128)(2,1)} %get-tuple-element.18), channel_id=1, source_target_pairs={{16,0},{32,16},{48,32},{64,48},{80,64},{96,80},{112,96},{0,112},{1... | collective-permute-start | bytes 221192 | tf_op jit(solution)/shard_map/ppermute | solution.py:401
  9.4 2.5 %collective-permute-done = bf16[288,128]{1,0:T(8,128)(2,1)S(1)} collective-permute-done((bf16[288,128]{1,0:T(8,128)(2,1)}, bf16[288,128]{1,0:T(8,128)(2,1)S(1)}, u32[]{:S(2)}, u32[]{:S(2)}) %collective-permute-start) | collective-permute-done | bytes 73760 | tf_op jit(solution)/shard_map/ppermute | solution.py:400
  12.9 1.7 %collective-permute-start.3 = (bf16[864,128]{1,0:T(8,128)(2,1)S(1)}, bf16[864,128]{1,0:T(8,128)(2,1)S(1)}, u32[]{:S(2)}, u32[]{:S(2)}) collective-permute-start(bf16[864,128]{1,0:T(8,128)(2,1)S(1)} %constant_dynamic-update-slice_fusion.x_own), channel_id=1, source_target_pairs={{1,0},{2,1},{3,2},{4,3},{5,4},{6,5},{7,6},{8,7},{9,8},{10,9},{11,1... | collective-permute-start | bytes 663560 | tf_op jit(solution)/shard_map/ppermute | solution.py:401
  14.6 2.2 %shard_map.175 = (s32[128,128]{1,0:T(8,128)}, bf16[352,1024]{1,0:T(8,128)(2,1)}, f32[16,512]{1,0:T(8,128)}, f32[16,384]{1,0:T(8,128)}) custom-call(s32[32,512]{1,0:T(8,128)} %neighbours.1, s32[32,512]{1,0:T(8,128)} %mask.1, f32[3,512]{1,0:T(4,128)} %frac.5, s32[3,32]{1,0:T(4,128)} %waves.1), custom_call_target="tpu_custom_call" | custom-call | flops 2000000000 | bytes 4000000 | tf_op jit(solution)/shard_map/pallas_call | solution.py:430
  16.8 2.1 %collective-permute-done.3.x_high = bf16[864,128]{1,0:T(8,128)(2,1)S(1)} collective-permute-done((bf16[864,128]{1,0:T(8,128)(2,1)S(1)}, bf16[864,128]{1,0:T(8,128)(2,1)S(1)}, u32[]{:S(2)}, u32[]{:S(2)}) %collective-permute-start.3) | collective-permute-done | bytes 221216 | tf_op jit(solution)/shard_map/ppermute | solution.py:401
  18.9 3.4 %collective-permute-done.2.x_low = bf16[864,128]{1,0:T(8,128)(2,1)S(1)} collective-permute-done((bf16[864,128]{1,0:T(8,128)(2,1)S(1)}, bf16[864,128]{1,0:T(8,128)(2,1)S(1)}, u32[]{:S(2)}, u32[]{:S(2)}) %collective-permute-start.2) | collective-permute-done | bytes 221216 | tf_op jit(solution)/shard_map/ppermute | solution.py:400
  23.0 23.0 %shard_map.177 = (bf16[512,128]{1,0:T(8,128)(2,1)}, bf16[512,128]{1,0:T(8,128)(2,1)}, bf16[256,128]{1,0:T(8,128)(2,1)}, f32[128,128]{1,0:T(8,128)}) custom-call(s32[16384]{0:T(1024)} %bitcast.5, s32[256]{0:T(256)} %send.3, s32[128,128]{1,0:T(8,128)} %get-tuple-element.17.slots, f32[3,512]{1,0:T(4,128)} %frac.5, bf16[864,128]{1,0:T(8,128)(2,1)} %copy-done.6, ...), custom_call_target="tpu_custom_call" | custom-call | flops 4000000000 | bytes 4000000 | tf_op jit(solution)/shard_map/pallas_call | solution.py:436
  46.0 3.4 %collective-permute-start.4 = (bf16[256,128]{1,0:T(8,128)(2,1)}, bf16[256,128]{1,0:T(8,128)(2,1)S(1)}, u32[]{:S(2)}, u32[]{:S(2)}) collective-permute-start(bf16[256,128]{1,0:T(8,128)(2,1)} %get-tuple-element.21), channel_id=1, source_target_pairs={{0,16},{16,32},{32,48},{48,64},{64,80},{80,96},{96,112},{112,0},{1... | collective-permute-start | bytes 196616 | tf_op jit(solution)/shard_map/ppermute | solution.py:400
  50.1 2.3 %collective-permute-start.5 = (bf16[256,128]{1,0:T(8,128)(2,1)}, bf16[256,128]{1,0:T(8,128)(2,1)S(1)}, u32[]{:S(2)}, u32[]{:S(2)}) collective-permute-start(bf16[256,128]{1,0:T(8,128)(2,1)} %get-tuple-element.21), channel_id=1, source_target_pairs={{16,0},{32,16},{48,32},{64,48},{80,64},{96,80},{112,96},{0,112},{1... | collective-permute-start | bytes 196616 | tf_op jit(solution)/shard_map/ppermute | solution.py:401
  52.4 1.7 %collective-permute-done.4 = bf16[256,128]{1,0:T(8,128)(2,1)S(1)} collective-permute-done((bf16[256,128]{1,0:T(8,128)(2,1)}, bf16[256,128]{1,0:T(8,128)(2,1)S(1)}, u32[]{:S(2)}, u32[]{:S(2)}) %collective-permute-start.4) | collective-permute-done | bytes 65568 | tf_op jit(solution)/shard_map/ppermute | solution.py:400
  56.7 13.7 %shard_map.178.filters = bf16[32,128,512]{2,1,0:T(8,128)(2,1)} custom-call(f32[128,128]{1,0:T(8,128)} %get-tuple-element.20.chord, bf16[2,32,128]{2,1,0:T(8,128)(2,1)} %w1.3, bf16[2,128,128]{2,1,0:T(8,128)(2,1)} %w2.3), custom_call_target="tpu_custom_call" | custom-call | flops 4000000000 | bytes 8000000 | tf_op jit(solution)/shard_map/pallas_call | solution.py:452
  71.1 16.9 %shard_map.179 = (bf16[512,128]{1,0:T(8,128)(2,1)}, bf16[128,384]{1,0:T(8,128)(2,1)}) custom-call(s32[16384]{0:T(1024)} %bitcast.6, bf16[32,128,512]{2,1,0:T(8,128)(2,1)} %shard_map.178.filters, bf16[768,128]{1,0:T(8,128)(2,1)} %copy-done.2, bf16[768,128]{1,0:T(8,128)(2,1)} %copy-done, bf16[768,128]{1,0:T(8,128)(2,1)} %copy-done.1, ...), custom_call_target="tpu_custom_call" | custom-call | flops 1000000000 | bytes 8000000 | tf_op jit(solution)/shard_map/pallas_call | solution.py:460
  88.1 1.6 %collective-permute-start.9 = (bf16[128,384]{1,0:T(8,128)(2,1)}, bf16[128,384]{1,0:T(8,128)(2,1)S(1)}, u32[]{:S(2)}, u32[]{:S(2)}) collective-permute-start(bf16[128,384]{1,0:T(8,128)(2,1)} %get-tuple-element.28), channel_id=1, source_target_pairs={{0,2},{1,3},{2,0},{3,1},{4,6},{5,7},{6,4},{7,5},{8,10},{9,11},{10,... | collective-permute-start | bytes 294920 | tf_op jit(solution)/shard_map/ppermute | solution.py:413
  89.9 3.3 %collective-permute-done.10 = bf16[128,384]{1,0:T(8,128)(2,1)S(1)} collective-permute-done((bf16[128,384]{1,0:T(8,128)(2,1)}, bf16[128,384]{1,0:T(8,128)(2,1)S(1)}, u32[]{:S(2)}, u32[]{:S(2)}) %collective-permute-start.10) | collective-permute-done | bytes 98336 | tf_op jit(solution)/shard_map/ppermute | solution.py:413
  93.2 2.3 %collective-permute-done.9 = bf16[128,384]{1,0:T(8,128)(2,1)S(1)} collective-permute-done((bf16[128,384]{1,0:T(8,128)(2,1)}, bf16[128,384]{1,0:T(8,128)(2,1)S(1)}, u32[]{:S(2)}, u32[]{:S(2)}) %collective-permute-start.9) | collective-permute-done | bytes 98336 | tf_op jit(solution)/shard_map/ppermute | solution.py:413
  98.4 2.2 %collective-permute-start.11 = (bf16[128,384]{1,0:T(8,128)(2,1)S(1)}, bf16[128,384]{1,0:T(8,128)(2,1)S(1)}, u32[]{:S(2)}, u32[]{:S(2)}) collective-permute-start(bf16[128,384]{1,0:T(8,128)(2,1)S(1)} %add_convert_fusion.3), channel_id=1, source_target_pairs={{0,4},{1,5},{2,6},{3,7},{4,0},{5,1},{6,2},{7,3},{8,12},{9,13},{10,... | collective-permute-start | bytes 294920 | tf_op jit(solution)/shard_map/ppermute | solution.py:413
  100.6 3.9 %collective-permute-done.13 = bf16[128,384]{1,0:T(8,128)(2,1)S(1)} collective-permute-done((bf16[128,384]{1,0:T(8,128)(2,1)S(1)}, bf16[128,384]{1,0:T(8,128)(2,1)S(1)}, u32[]{:S(2)}, u32[]{:S(2)}) %collective-permute-start.13) | collective-permute-done | bytes 98336 | tf_op jit(solution)/shard_map/ppermute | solution.py:413
  105.1 3.7 %collective-permute-start.16 = (bf16[128,384]{1,0:T(8,128)(2,1)S(1)}, bf16[128,384]{1,0:T(8,128)(2,1)S(1)}, u32[]{:S(2)}, u32[]{:S(2)}) collective-permute-start(bf16[128,384]{1,0:T(8,128)(2,1)S(1)} %add_convert_fusion.2), channel_id=1, source_target_pairs={{0,48},{16,32},{32,16},{48,0},{64,112},{80,96},{96,80},{112,64},{1... | collective-permute-start | bytes 294920 | tf_op jit(solution)/shard_map/ppermute | solution.py:413
  110.2 2.6 %collective-permute-done.16 = bf16[128,384]{1,0:T(8,128)(2,1)S(1)} collective-permute-done((bf16[128,384]{1,0:T(8,128)(2,1)S(1)}, bf16[128,384]{1,0:T(8,128)(2,1)S(1)}, u32[]{:S(2)}, u32[]{:S(2)}) %collective-permute-start.16) | collective-permute-done | bytes 98336 | tf_op jit(solution)/shard_map/ppermute | solution.py:413
  115.0 3.8 %collective-permute-start.17 = (bf16[128,384]{1,0:T(8,128)(2,1)S(1)}, bf16[128,384]{1,0:T(8,128)(2,1)S(1)}, u32[]{:S(2)}, u32[]{:S(2)}) collective-permute-start(bf16[128,384]{1,0:T(8,128)(2,1)S(1)} %add_convert_fusion.1), channel_id=1, source_target_pairs={{0,64},{16,80},{32,96},{48,112},{64,0},{80,16},{96,32},{112,48},{1... | collective-permute-start | bytes 294920 | tf_op jit(solution)/shard_map/ppermute | solution.py:413
  118.7 2.6 %collective-permute-done.17 = bf16[128,384]{1,0:T(8,128)(2,1)S(1)} collective-permute-done((bf16[128,384]{1,0:T(8,128)(2,1)S(1)}, bf16[128,384]{1,0:T(8,128)(2,1)S(1)}, u32[]{:S(2)}, u32[]{:S(2)}) %collective-permute-start.17) | collective-permute-done | bytes 98336 | tf_op jit(solution)/shard_map/ppermute | solution.py:413
  122.0 2.6 %shard_map.180 = (f32[16,512]{1,0:T(8,128)}, f32[1,512]{1,0:T(1,128)}) custom-call(bf16[128,384]{1,0:T(8,128)(2,1)} %add_convert_fusion.sums, bf16[352,1024]{1,0:T(8,128)(2,1)} %get-tuple-element.24.phase, f32[16,512]{1,0:T(8,128)} %get-tuple-element.25.axis, f32[1,16]{1,0:T(1,128)} %bitcast.8, bf16[512,128]{1,0:T(8,128)(2,1)} %get-tuple-element.14.state, ...), custom_call_target="tpu_custom_call" | custom-call | flops 100000000 | bytes 2000000 | tf_op jit(solution)/shard_map/pallas_call | solution.py:469
  (43 shorter events, 13.7 us)
Async XLA Ops:
  2.8 9.1 %collective-permute-start = (bf16[288,128]{1,0:T(8,128)(2,1)}, bf16[288,128]{1,0:T(8,128)(2,1)S(1)}, u32[]{:S(2)}, u32[]{:S(2)}) collective-permute-start(bf16[288,128]{1,0:T(8,128)(2,1)} %get-tuple-element.18), channel_id=1, source_target_pairs={{0,16},{16,32},{32,48},{48,64},{64,80},{80,96},{96,112},{112,0},{1... | collective-permute-start | bytes 221192 | tf_op jit(solution)/shard_map/ppermute | solution.py:400
  5.9 6.9 %collective-permute-start.1 = (bf16[288,128]{1,0:T(8,128)(2,1)}, bf16[288,128]{1,0:T(8,128)(2,1)S(1)}, u32[]{:S(2)}, u32[]{:S(2)}) collective-permute-start(bf16[288,128]{1,0:T(8,128)(2,1)} %get-tuple-element.18), channel_id=1, source_target_pairs={{16,0},{32,16},{48,32},{64,48},{80,64},{96,80},{112,96},{0,112},{1... | collective-permute-start | bytes 221192 | tf_op jit(solution)/shard_map/ppermute | solution.py:401
  12.9 9.4 %copy-start.3 = (bf16[864,128]{1,0:T(8,128)(2,1)}, bf16[864,128]{1,0:T(8,128)(2,1)S(1)}, u32[]{:S(2)}) copy-start(bf16[864,128]{1,0:T(8,128)(2,1)S(1)} %constant_dynamic-update-slice_fusion.x_own) | copy-start | bytes 663556
  12.9 6.0 %collective-permute-start.3 = (bf16[864,128]{1,0:T(8,128)(2,1)S(1)}, bf16[864,128]{1,0:T(8,128)(2,1)S(1)}, u32[]{:S(2)}, u32[]{:S(2)}) collective-permute-start(bf16[864,128]{1,0:T(8,128)(2,1)S(1)} %constant_dynamic-update-slice_fusion.x_own), channel_id=1, source_target_pairs={{1,0},{2,1},{3,2},{4,3},{5,4},{6,5},{7,6},{8,7},{9,8},{10,9},{11,1... | collective-permute-start | bytes 663560 | tf_op jit(solution)/shard_map/ppermute | solution.py:401
  14.6 7.7 %collective-permute-start.2 = (bf16[864,128]{1,0:T(8,128)(2,1)S(1)}, bf16[864,128]{1,0:T(8,128)(2,1)S(1)}, u32[]{:S(2)}, u32[]{:S(2)}) collective-permute-start(bf16[864,128]{1,0:T(8,128)(2,1)S(1)} %constant_dynamic-update-slice_fusion.x_own), channel_id=1, source_target_pairs={{0,1},{1,2},{2,3},{3,4},{4,5},{5,6},{6,7},{7,8},{8,9},{9,10},{10,1... | collective-permute-start | bytes 663560 | tf_op jit(solution)/shard_map/ppermute | solution.py:400
  18.9 3.4 %copy-start.5 = (bf16[864,128]{1,0:T(8,128)(2,1)}, bf16[864,128]{1,0:T(8,128)(2,1)S(1)}, u32[]{:S(2)}) copy-start(bf16[864,128]{1,0:T(8,128)(2,1)S(1)} %collective-permute-done.3.x_high) | copy-start | bytes 663556
  23.0 26.4 %copy-start.4 = (bf16[128,16]{0,1:T(8,128)(2,1)S(1)}, bf16[128,16]{0,1:T(8,128)(2,1)}, u32[]{:S(2)}) copy-start(bf16[128,16]{0,1:T(8,128)(2,1)} %param.27) | copy-start | bytes 12292
  46.0 8.1 %collective-permute-start.4 = (bf16[256,128]{1,0:T(8,128)(2,1)}, bf16[256,128]{1,0:T(8,128)(2,1)S(1)}, u32[]{:S(2)}, u32[]{:S(2)}) collective-permute-start(bf16[256,128]{1,0:T(8,128)(2,1)} %get-tuple-element.21), channel_id=1, source_target_pairs={{0,16},{16,32},{32,48},{48,64},{64,80},{80,96},{96,112},{112,0},{1... | collective-permute-start | bytes 196616 | tf_op jit(solution)/shard_map/ppermute | solution.py:400
  50.1 6.0 %collective-permute-start.5 = (bf16[256,128]{1,0:T(8,128)(2,1)}, bf16[256,128]{1,0:T(8,128)(2,1)S(1)}, u32[]{:S(2)}, u32[]{:S(2)}) collective-permute-start(bf16[256,128]{1,0:T(8,128)(2,1)} %get-tuple-element.21), channel_id=1, source_target_pairs={{16,0},{32,16},{48,32},{64,48},{80,64},{96,80},{112,96},{0,112},{1... | collective-permute-start | bytes 196616 | tf_op jit(solution)/shard_map/ppermute | solution.py:401
  56.1 14.3 %copy-start = (bf16[768,128]{1,0:T(8,128)(2,1)}, bf16[768,128]{1,0:T(8,128)(2,1)S(1)}, u32[]{:S(2)}) copy-start(bf16[768,128]{1,0:T(8,128)(2,1)S(1)} %constant_dynamic-update-slice_fusion.3.x_own) | copy-start | bytes 589828
  56.1 14.3 %collective-permute-start.7 = (bf16[768,128]{1,0:T(8,128)(2,1)S(1)}, bf16[768,128]{1,0:T(8,128)(2,1)S(1)}, u32[]{:S(2)}, u32[]{:S(2)}) collective-permute-start(bf16[768,128]{1,0:T(8,128)(2,1)S(1)} %constant_dynamic-update-slice_fusion.3.x_own), channel_id=1, source_target_pairs={{1,0},{2,1},{3,2},{4,3},{5,4},{6,5},{7,6},{8,7},{9,8},{10,9},{11,1... | collective-permute-start | bytes 589832 | tf_op jit(solution)/shard_map/ppermute | solution.py:401
  56.2 14.2 %collective-permute-start.6 = (bf16[768,128]{1,0:T(8,128)(2,1)S(1)}, bf16[768,128]{1,0:T(8,128)(2,1)S(1)}, u32[]{:S(2)}, u32[]{:S(2)}) collective-permute-start(bf16[768,128]{1,0:T(8,128)(2,1)S(1)} %constant_dynamic-update-slice_fusion.3.x_own), channel_id=1, source_target_pairs={{0,1},{1,2},{2,3},{3,4},{4,5},{5,6},{6,7},{7,8},{8,9},{9,10},{10,1... | collective-permute-start | bytes 589832 | tf_op jit(solution)/shard_map/ppermute | solution.py:400
  70.4 0.7 copy-start.1
  70.4 0.8 copy-start.2
  88.0 5.1 %collective-permute-start.10 = (bf16[128,384]{1,0:T(8,128)(2,1)}, bf16[128,384]{1,0:T(8,128)(2,1)S(1)}, u32[]{:S(2)}, u32[]{:S(2)}) collective-permute-start(bf16[128,384]{1,0:T(8,128)(2,1)} %get-tuple-element.28), channel_id=1, source_target_pairs={{0,3},{1,2},{2,1},{3,0},{4,7},{5,6},{6,5},{7,4},{8,11},{9,10},{10,... | collective-permute-start | bytes 294920 | tf_op jit(solution)/shard_map/ppermute | solution.py:413
  88.1 7.4 %collective-permute-start.9 = (bf16[128,384]{1,0:T(8,128)(2,1)}, bf16[128,384]{1,0:T(8,128)(2,1)S(1)}, u32[]{:S(2)}, u32[]{:S(2)}) collective-permute-start(bf16[128,384]{1,0:T(8,128)(2,1)} %get-tuple-element.28), channel_id=1, source_target_pairs={{0,2},{1,3},{2,0},{3,1},{4,6},{5,7},{6,4},{7,5},{8,10},{9,11},{10,... | collective-permute-start | bytes 294920 | tf_op jit(solution)/shard_map/ppermute | solution.py:413
  89.7 5.8 %collective-permute-start.8 = (bf16[128,384]{1,0:T(8,128)(2,1)}, bf16[128,384]{1,0:T(8,128)(2,1)S(1)}, u32[]{:S(2)}, u32[]{:S(2)}) collective-permute-start(bf16[128,384]{1,0:T(8,128)(2,1)} %get-tuple-element.28), channel_id=1, source_target_pairs={{0,1},{1,0},{2,3},{3,2},{4,5},{5,4},{6,7},{7,6},{8,9},{9,8},{10,11... | collective-permute-start | bytes 294920 | tf_op jit(solution)/shard_map/ppermute | solution.py:413
  96.4 8.0 %collective-permute-start.13 = (bf16[128,384]{1,0:T(8,128)(2,1)S(1)}, bf16[128,384]{1,0:T(8,128)(2,1)S(1)}, u32[]{:S(2)}, u32[]{:S(2)}) collective-permute-start(bf16[128,384]{1,0:T(8,128)(2,1)S(1)} %add_convert_fusion.3), channel_id=1, source_target_pairs={{0,12},{1,13},{2,14},{3,15},{4,8},{5,9},{6,10},{7,11},{8,4},{9,5},... | collective-permute-start | bytes 294920 | tf_op jit(solution)/shard_map/ppermute | solution.py:413
  97.9 6.5 %collective-permute-start.12 = (bf16[128,384]{1,0:T(8,128)(2,1)S(1)}, bf16[128,384]{1,0:T(8,128)(2,1)S(1)}, u32[]{:S(2)}, u32[]{:S(2)}) collective-permute-start(bf16[128,384]{1,0:T(8,128)(2,1)S(1)} %add_convert_fusion.3), channel_id=1, source_target_pairs={{0,8},{1,9},{2,10},{3,11},{4,12},{5,13},{6,14},{7,15},{8,0},{9,1},... | collective-permute-start | bytes 294920 | tf_op jit(solution)/shard_map/ppermute | solution.py:413
  98.4 6.7 %collective-permute-start.11 = (bf16[128,384]{1,0:T(8,128)(2,1)S(1)}, bf16[128,384]{1,0:T(8,128)(2,1)S(1)}, u32[]{:S(2)}, u32[]{:S(2)}) collective-permute-start(bf16[128,384]{1,0:T(8,128)(2,1)S(1)} %add_convert_fusion.3), channel_id=1, source_target_pairs={{0,4},{1,5},{2,6},{3,7},{4,0},{5,1},{6,2},{7,3},{8,12},{9,13},{10,... | collective-permute-start | bytes 294920 | tf_op jit(solution)/shard_map/ppermute | solution.py:413
  105.1 7.6 %collective-permute-start.16 = (bf16[128,384]{1,0:T(8,128)(2,1)S(1)}, bf16[128,384]{1,0:T(8,128)(2,1)S(1)}, u32[]{:S(2)}, u32[]{:S(2)}) collective-permute-start(bf16[128,384]{1,0:T(8,128)(2,1)S(1)} %add_convert_fusion.2), channel_id=1, source_target_pairs={{0,48},{16,32},{32,16},{48,0},{64,112},{80,96},{96,80},{112,64},{1... | collective-permute-start | bytes 294920 | tf_op jit(solution)/shard_map/ppermute | solution.py:413
  108.8 4.8 %collective-permute-start.15 = (bf16[128,384]{1,0:T(8,128)(2,1)S(1)}, bf16[128,384]{1,0:T(8,128)(2,1)S(1)}, u32[]{:S(2)}, u32[]{:S(2)}) collective-permute-start(bf16[128,384]{1,0:T(8,128)(2,1)S(1)} %add_convert_fusion.2), channel_id=1, source_target_pairs={{0,32},{16,48},{32,0},{48,16},{64,96},{80,112},{96,64},{112,80},{1... | collective-permute-start | bytes 294920 | tf_op jit(solution)/shard_map/ppermute | solution.py:413
  108.8 6.1 %collective-permute-start.14 = (bf16[128,384]{1,0:T(8,128)(2,1)S(1)}, bf16[128,384]{1,0:T(8,128)(2,1)S(1)}, u32[]{:S(2)}, u32[]{:S(2)}) collective-permute-start(bf16[128,384]{1,0:T(8,128)(2,1)S(1)} %add_convert_fusion.2), channel_id=1, source_target_pairs={{0,16},{16,0},{32,48},{48,32},{64,80},{80,64},{96,112},{112,96},{1... | collective-permute-start | bytes 294920 | tf_op jit(solution)/shard_map/ppermute | solution.py:413
  115.0 6.3 %collective-permute-start.17 = (bf16[128,384]{1,0:T(8,128)(2,1)S(1)}, bf16[128,384]{1,0:T(8,128)(2,1)S(1)}, u32[]{:S(2)}, u32[]{:S(2)}) collective-permute-start(bf16[128,384]{1,0:T(8,128)(2,1)S(1)} %add_convert_fusion.1), channel_id=1, source_target_pairs={{0,64},{16,80},{32,96},{48,112},{64,0},{80,16},{96,32},{112,48},{1... | collective-permute-start | bytes 294920 | tf_op jit(solution)/shard_map/ppermute | solution.py:413
  (1 other events, 0.7 us)

commit v2 on v1

--- a/solution.py
+++ b/solution.py
@@ -25,6 +25,7 @@
 ROWS = KX * Q
 SUM_ROWS = ROWS + 16
 SUM_LANES = 384
+HALF = SUM_ROWS // 2
 f32, bf16, i32 = jnp.float32, jnp.bfloat16, jnp.int32
 
 
@@ -182,16 +183,24 @@
         wide2[j * C : (j + 1) * C, j * C : (j + 1) * C] = w2[layer]
 
 
-def filters_of(chord_rows, wide1, wide2):
-    inv_width = 31.0 / 3.0
-    centre = rows_of((NR, 128), 0).astype(f32)
-    radial = []
-    for chord in chord_rows:
-        scaled = chord * inv_width - centre
-        radial.append(jnp.exp(-0.5 * scaled * scaled))
-    radial = jnp.concatenate(radial, axis=0).astype(bf16)
-    hidden = silu(dot(radial, wide1[...], ((0,), (0,)))).astype(bf16)
-    return (dot(hidden[:, : 2 * C], wide2[...]), dot(hidden[:, 2 * C :], wide2[...]))
+def radial_of(chord):
+    scaled = chord * (31.0 / 3.0) - rows_of((NR, 128), 0).astype(f32)
+    return jnp.exp(-0.5 * scaled * scaled).astype(bf16)
+
+
+def make_filters(chord, group, wide1, wide2, out):
+    radial = jnp.concatenate(
+        [
+            jnp.concatenate(
+                [radial_of(chord[pl.ds(b * K + group * 4 + j, NR, stride=0), :]) for b in range(T // 128)], axis=1
+            )
+            for j in range(4)
+        ],
+        axis=0,
+    )
+    for h in range(2):
+        hidden = silu(dot(radial, wide1[:, h * 2 * C : (h + 1) * 2 * C], ((0,), (0,)))).astype(bf16)
+        out[h] = dot(hidden, wide2[...]).astype(bf16)
 
 
 def update_tail(total, state, w_update1, w_update2, layer):
@@ -239,21 +248,25 @@
 
 def add_messages(table, slots, filters, total, block, group):
     first = block * (K * 128) + group * 512
-    for g in range(16):
-        start = block * 128 + g * 8
-        at = pl.ds(pl.multiple_of(start, 8), 8)
+    ahead = [slots.at[pl.ds(c, K * T - 512)] for c in range(512)]
+    for g in range(8):
+        at = pl.ds(pl.multiple_of(block * 128 + g * 16, 16), 16)
         acc = total[at, :]
+        parts = [acc[:8], acc[8:]]
         for j in range(4):
-            source = pick8(table, lambda s: slots[first + (j * 128 + g * 8 + s)])
-            acc = acc + source * filters[g * 8 : g * 8 + 8, j * C : (j + 1) * C]
-        total[at, :] = acc
+            weight = filters[j // 2, at, (j % 2) * C : (j % 2 + 1) * C].astype(f32)
+            for n in range(2):
+                c = j * 128 + g * 16 + n * 8
+                source = pick8(table, lambda s: ahead[c + s][first])
+                parts[n] = parts[n] + source * weight[n * 8 : n * 8 + 8]
+        total[at, :] = jnp.concatenate(parts, axis=0)
 
 
 def layer_kernel(
     slots_s, send, slots, frac, x_low, x_own, x_high, projected, state,
     w1, w2, w_update1, w_update2, w_in,
     state_out, proj_out, send_out, chord_out,
-    table, places, wide1, wide2, ping, pong, total, proj_table,
+    table, places, wide1, wide2, filters, total, proj_table,
 ):
     rows_in = (x_low, x_own, x_high)
     fill_table(table, projected, rows_in, PACK)
@@ -261,26 +274,16 @@
     chords(slots, frac, rows_in, chord_out, places)
     total[...] = jnp.zeros_like(total)
 
-    def make(step, buffer):
-        block, group = step // 8, step % 8
-        rows = [chord_out[pl.ds(block * K + group * 4 + j, NR, stride=0), :] for j in range(4)]
-        a, b = filters_of(rows, wide1, wide2)
-        buffer[:, : 2 * C] = a
-        buffer[:, 2 * C :] = b
-
-    def use(step, buffer):
-        add_messages(table, slots_s, buffer, total, step // 8, step % 8)
-
-    make(0, ping)
-
-    def pair(i, carry):
-        make(2 * i + 1, pong)
-        use(2 * i, ping)
-        make(jnp.minimum(2 * i + 2, 31), ping)
-        use(2 * i + 1, pong)
+    def make(group, carry):
+        make_filters(chord_out, group, wide1, wide2, filters.at[group])
         return carry
 
-    lax.fori_loop(0, 16, pair, 0)
+    def use(i, carry):
+        add_messages(table, slots_s, filters.at[i // 4], total, i % 4, i // 4)
+        return carry
+
+    lax.fori_loop(0, 8, make, 0)
+    lax.fori_loop(0, 32, use, 0)
     new_state = update_tail(total, state, w_update1, w_update2, 0)
     state_out[...] = new_state
     projected1 = dot(new_state, w_in[1]).astype(bf16)
@@ -290,65 +293,68 @@
 
 
 def filter_kernel(chord, w1, w2, out, wide1, wide2):
-    @pl.when(pl.program_id(0) == 0)
+    step = pl.program_id(0)
+
+    @pl.when(step == 0)
     def _():
         fill_filter_weights(w1, w2, 1, wide1, wide2)
 
-    first = pl.program_id(0) * K
-
-    def group(g, carry):
-        rows = [chord[pl.ds(first + g * 4 + j, NR, stride=0), :] for j in range(4)]
-        a, b = filters_of(rows, wide1, wide2)
-        out[g, :, : 2 * C] = a.astype(bf16)
-        out[g, :, 2 * C :] = b.astype(bf16)
+    def make(i, carry):
+        make_filters(chord, step * 2 + i, wide1, wide2, out.at[i])
         return carry
 
-    lax.fori_loop(0, 8, group, 0)
+    lax.fori_loop(0, 2, make, 0)
 
 
 def last_layer_kernel(
-    slots_s, filters, x_low, x_own, x_high, projected, state,
+    slots_s, core, filters, x_low, x_own, x_high, projected, state,
     w_update1, w_update2, w_charge, phase, axis, digits,
-    state_out, sums_out,
-    table, total, left,
+    state_out, keep_out, give_out,
+    table, total, left, sums,
 ):
-    block = pl.program_id(0)
-
-    @pl.when(block == 0)
+    step = pl.program_id(0)
+
+    @pl.when(step == 0)
     def _():
         fill_table(table, projected, (x_low, x_own, x_high), H)
         total[...] = jnp.zeros_like(total)
 
-    def group(g, carry):
-        add_messages(table, slots_s, filters.at[g], total, block, g)
+    def use(i, carry):
+        add_messages(table, slots_s, filters.at[i // 4], total, i % 4, step * 2 + i // 4)
         return carry
 
-    lax.fori_loop(0, 8, group, 0)
-
-    @pl.when(block == T // 128 - 1)
+    lax.fori_loop(0, 8, use, 0)
+
+    @pl.when(step == 3)
     def _():
         new_state = update_tail(total, state, w_update1, w_update2, 1)
         state_out[...] = new_state
-        charges = dot(w_charge[...], new_state, ((0,), (1,))).astype(bf16).astype(f32)
+        charges = dot(w_charge[...], new_state, ((1,), (1,))).astype(bf16).astype(f32)
         for n in range(KX):
             left[n * Q : (n + 1) * Q, :T] = (charges * axis[n : n + 1, :]).astype(bf16)
             left[n * Q : (n + 1) * Q, T:] = (charges * axis[8 + n : 9 + n, :]).astype(bf16)
-        sums_out[...] = jnp.zeros_like(sums_out)
-        sums_out[:ROWS, : 2 * BETA] = dot(left[...], phase[...], ((1,), (1,))).astype(bf16)
-        sums_out[ROWS:, :] = digits[...].astype(bf16)
+        sums[...] = jnp.zeros_like(sums)
+        sums[:ROWS, : 2 * BETA] = dot(left[...], phase[...], ((1,), (1,)))
+        sums[ROWS:, :] = digits[...]
+        mine = pl.multiple_of(core[0] * HALF, HALF)
+        keep_out[...] = sums[pl.ds(mine, HALF), :].astype(bf16)
+        give_out[...] = sums[pl.ds(pl.multiple_of(HALF - mine, HALF), HALF), :].astype(bf16)
 
 
 def field_kernel(
-    sums, phase, axis, screening, state, w_head, w_potential, w_energy,
-    potentials_out, energies_out, response,
+    core, own_half, other_half, phase, axis, screening, state, w_head, w_potential, w_energy,
+    potentials_out, energies_out, response, sums,
 ):
+    mine = pl.multiple_of(core[0] * HALF, HALF)
+    sums[pl.ds(mine, HALF), :] = own_half[...].astype(f32)
+    sums[pl.ds(pl.multiple_of(HALF - mine, HALF), HALF), :] = other_half[...].astype(f32)
     lane = rows_of((1, SUM_LANES), 1)
     beta = jnp.where(lane >= BETA, lane - BETA, lane)
     y = (beta * 79) >> 10
     ky = y - 6
     kz = beta - y * YZ - 6
     plane_sq = (ky * ky + kz * kz).astype(f32)
-    digits = sums[ROWS:, :].astype(f32)
+    digits = sums[ROWS:, :]
     packed = digits[0:8] + 3.0 * digits[8:16]
     ahead = pltpu.roll(packed, SUM_LANES - BETA, 1)
     behind = pltpu.roll(packed, BETA, 1)
@@ -359,7 +365,7 @@
     for n in range(KX):
         norm_sq = plane_sq + float(n * n)
         kernel = jnp.exp(norm_sq * (-1.0 / 64.0)) * count[n : n + 1, :] / (norm_sq + screen)
-        value = kernel * sums[n * Q : (n + 1) * Q, :].astype(f32)
+        value = kernel * sums[n * Q : (n + 1) * Q, :]
         response[n * Q : (n + 1) * Q, :] = value[:, : 2 * BETA].astype(bf16)
     field = dot(response[...], phase[...])
     total = jnp.zeros((Q, T), f32)
@@ -404,18 +410,23 @@
     return low, block, high
 
 
-STAGES = (("yz", (1, 2, 3)), ("yz", (4, 8, 12)), ("gx", (1, 2, 3)), ("gx", (4,)))
-
-
-def sum_everywhere(part):
-    for axis, offsets in STAGES:
-        count = lax.axis_size(axis)
-        taken = [lax.ppermute(part, axis, [(i, i ^ o) for i in range(count)]) for o in offsets]
+RINGS = ((2, 16, 18), (4, 8, 12), (32, 64, 96))
+
+
+def exchange(part, offset):
+    count = lax.axis_size("gx") * lax.axis_size("yz")
+    return lax.ppermute(part, ("gx", "yz"), [(i, i ^ offset) for i in range(count)])
+
+
+def sum_everywhere(keep, give):
+    part = (keep.astype(f32) + exchange(give, 1).astype(f32)).astype(bf16)
+    for offsets in RINGS:
+        taken = [exchange(part, o) for o in offsets]
         total = part.astype(f32)
         for one in taken:
             total = total + one.astype(f32)
         part = total.astype(bf16)
-    return part
+    return part, exchange(part, 1)
 
 
 def shards(
@@ -439,7 +450,7 @@
         [
             pltpu.VMEM((SLOTS + 8, C), f32), pltpu.VMEM((72, 128), f32),
             pltpu.VMEM((4 * NR, 4 * C), bf16), pltpu.VMEM((2 * C, 2 * C), bf16),
-            pltpu.VMEM((128, 4 * C), f32), pltpu.VMEM((128, 4 * C), f32),
+            pltpu.VMEM((8, 2, T, 2 * C), bf16),
             pltpu.VMEM((T, C), f32), pltpu.VMEM((T, C), f32),
         ], 4_000_000_000, 4_000_000,
     )(
@@ -448,29 +459,35 @@
     )
     x_low, x_own, x_high = halo(sent)
     whole = lambda a: pl.BlockSpec(a.shape, lambda i: (0,) * a.ndim)
-    block = pl.BlockSpec((8, 128, 4 * C), lambda i: (i, 0, 0))
+    block = pl.BlockSpec((2, 2, T, 2 * C), lambda i: (i, 0, 0, 0))
     filters = pl.pallas_call(
-        filter_kernel, grid=(T // 128,),
-        out_shape=shape(32, 128, 4 * C, dtype=bf16),
+        filter_kernel, grid=(4,),
+        out_shape=shape(8, 2, T, 2 * C, dtype=bf16),
         in_specs=[whole(chord), whole(w_filter1), whole(w_filter2)], out_specs=block,
         scratch_shapes=[pltpu.VMEM((4 * NR, 4 * C), bf16), pltpu.VMEM((2 * C, 2 * C), bf16)],
         cost_estimate=pl.CostEstimate(flops=4_000_000_000, bytes_accessed=8_000_000, transcendentals=0),
     )(chord, w_filter1, w_filter2)
-    rest = (x_low, x_own, x_high, projected, state, w_update1, w_update2, w_charge, phase, axis, digits)
-    embeddings, sums = pl.pallas_call(
-        last_layer_kernel, grid=(T // 128,),
-        out_shape=(shape(T, C, dtype=bf16), shape(SUM_ROWS, SUM_LANES, dtype=bf16)),
-        in_specs=[SMEM, block] + [whole(a) for a in rest],
-        out_specs=(pl.BlockSpec((T, C), lambda i: (0, 0)), pl.BlockSpec((SUM_ROWS, SUM_LANES), lambda i: (0, 0))),
-        scratch_shapes=[pltpu.VMEM((SLOTS + 8, C), f32), pltpu.VMEM((T, C), f32), pltpu.VMEM((ROWS, 2 * T), bf16)],
+    rest = (x_low, x_own, x_high, projected, state, w_update1, w_update2, w_charge.T, phase, axis, digits)
+    half = shape(HALF, SUM_LANES, dtype=bf16)
+    half_spec = pl.BlockSpec(half.shape, lambda i: (0, 0))
+    core = (lax.axis_index("yz") & 1).reshape(1)
+    embeddings, keep, give = pl.pallas_call(
+        last_layer_kernel, grid=(4,),
+        out_shape=(shape(T, C, dtype=bf16), half, half),
+        in_specs=[SMEM, SMEM, block] + [whole(a) for a in rest],
+        out_specs=(pl.BlockSpec((T, C), lambda i: (0, 0)), half_spec, half_spec),
+        scratch_shapes=[
+            pltpu.VMEM((SLOTS + 8, C), f32), pltpu.VMEM((T, C), f32), pltpu.VMEM((ROWS, 2 * T), bf16),
+            pltpu.VMEM((SUM_ROWS, SUM_LANES), f32),
+        ],
         cost_estimate=pl.CostEstimate(flops=1_000_000_000, bytes_accessed=8_000_000, transcendentals=0),
-    )(slots.reshape(-1), filters, *rest)
-    sums = sum_everywhere(sums)
+    )(slots.reshape(-1), core, filters, *rest)
+    own_half, other_half = sum_everywhere(keep, give)
     potentials, energies = call(
-        field_kernel, [VMEM] * 8, (shape(Q, T), shape(1, T)),
-        [pltpu.VMEM((ROWS, 2 * BETA), bf16)], 100_000_000, 2_000_000,
+        field_kernel, [SMEM] + [VMEM] * 9, (shape(Q, T), shape(1, T)),
+        [pltpu.VMEM((ROWS, 2 * BETA), bf16), pltpu.VMEM((SUM_ROWS, SUM_LANES), f32)], 100_000_000, 2_000_000,
     )(
-        sums, phase, axis, screening.reshape(1, Q), embeddings, w_head, w_potential,
+        core, own_half, other_half, phase, axis, screening.reshape(1, Q), embeddings, w_head, w_potential,
         w_energy.reshape(1, C),
     )
     return embeddings, potentials, energies.reshape(T)

time: 125 us -> 106 us (0.85)
  Pallas kernels: 60.5 us -> 46.6 us
  waiting for transfers between devices: 28.2 us -> 25.7 us
  starting transfers between devices: 29.4 us -> 27.3 us
    pallas_call x3, Pallas kernels: 33.2 us -> 22.7 us  [the longest x1 13.4 us: shards(): pl.pallas_call(last_layer_kernel, grid=(4,), out_shape=(shape(T, C, dtype...]
    pallas_call x1, Pallas kernels: 23 us -> 19.5 us  [shards(): call(layer_kernel, [SMEM, SMEM] + [VMEM] * 12, (shape(T, C, dtype=bf16),...]
    ppermute x10 -> x11, waiting for transfers between devices: 17.3 us -> 14.6 us  [exchange(): lax.ppermute(part, ('gx', 'yz'), [(i, i ^ offset) for i in range(count)])]
    ppermute x10 -> x11, starting transfers between devices: 14.9 us -> 12.8 us  [exchange(): lax.ppermute(part, ('gx', 'yz'), [(i, i ^ offset) for i in range(count)])]
    convert_element_type x4 -> x3, other arithmetic: 1.72 us -> 0.09 us  [sum_everywhere(): part = total.astype(bf16)]
    unnamed x19 -> x20, local copies, waits for them, and re-layouts: 3.93 us -> 3.76 us
  transfers between devices with their start and end apart: 18 -> 19, of which waited for: 13 -> 14; matrix products, arithmetic and copies ran while one was open for 2% -> 2% of each run, Pallas kernels for 13% -> 8%
where the time goes in v2:
time: 106 us; the launch traced here: 105 us
  Pallas kernels  46.6 us (44%)
  starting transfers between devices  27.3 us (26%)
  waiting for transfers between devices  25.7 us (24%)
  local copies, waits for them, and re-layouts  3.78 us (4%)
    pallas_call x1, Pallas kernels, shards(): call(layer_kernel, [SMEM, SMEM] + [VMEM] * 12, (shape(T, C, dtype=bf16),...  19.5 us
    ppermute x11, waiting for transfers between devices, exchange(): lax.ppermute(part, ('gx', 'yz'), [(i, i ^ offset) for i in range(count)])  14.6 us
    pallas_call x1, Pallas kernels, shards(): pl.pallas_call(last_layer_kernel, grid=(4,), out_shape=(shape(T, C, dtype...  13.4 us
    ppermute x11, starting transfers between devices, exchange(): lax.ppermute(part, ('gx', 'yz'), [(i, i ^ offset) for i in range(count)])  12.8 us
    ppermute x4, waiting for transfers between devices, halo(): low = lax.ppermute(block, axis, forward)  8.54 us
    ppermute x4, starting transfers between devices, halo(): high = lax.ppermute(block, axis, backward)  7.51 us
    ppermute x4, starting transfers between devices, halo(): low = lax.ppermute(block, axis, forward)  7 us
    pallas_call x1, Pallas kernels, shards(): pl.pallas_call(filter_kernel, grid=(4,), out_shape=shape(8, 2, T, 2 * C,...  6.61 us
  transfers between devices with their start and end apart: 19, of which 14 were waited for; matrix products, arithmetic and copies ran while one was open for 2% of the time, Pallas kernels for 8%

profile of v2, /device:TPU:0, one launch (start us, length us, event | category | flops | bytes accessed | tf_op | source)
XLA Modules:
  0.0 105.0 jit_solution(16917186468850841725)
XLA Ops:
  0.6 2.2 %shard_map.176 = (bf16[512,128]{1,0:T(8,128)(2,1)}, bf16[288,128]{1,0:T(8,128)(2,1)}) custom-call(s32[256]{0:T(256)} %send.3, s32[2,128]{1,0:T(2,128)} %bitcast.9, bf16[512,128]{1,0:T(8,128)(2,1)} %state.1, f32[3,512]{1,0:T(4,128)} %frac.5, bf16[2,128,128]{2,1,0:T(8,128)(2,1)} %w_in.3), custom_call_target="tpu_custom_call" | custom-call | flops 20000000 | bytes 300000 | tf_op jit(solution)/shard_map/pallas_call | solution.py:436
  2.8 3.1 %collective-permute-start = (bf16[288,128]{1,0:T(8,128)(2,1)}, bf16[288,128]{1,0:T(8,128)(2,1)S(1)}, u32[]{:S(2)}, u32[]{:S(2)}) collective-permute-start(bf16[288,128]{1,0:T(8,128)(2,1)} %get-tuple-element.19), channel_id=1, source_target_pairs={{0,16},{16,32},{32,48},{48,64},{64,80},{80,96},{96,112},{112,0},{1... | collective-permute-start | bytes 221192 | tf_op jit(solution)/shard_map/ppermute | solution.py:406
  5.9 3.5 %collective-permute-start.1 = (bf16[288,128]{1,0:T(8,128)(2,1)}, bf16[288,128]{1,0:T(8,128)(2,1)S(1)}, u32[]{:S(2)}, u32[]{:S(2)}) collective-permute-start(bf16[288,128]{1,0:T(8,128)(2,1)} %get-tuple-element.19), channel_id=1, source_target_pairs={{16,0},{32,16},{48,32},{64,48},{80,64},{96,80},{112,96},{0,112},{1... | collective-permute-start | bytes 221192 | tf_op jit(solution)/shard_map/ppermute | solution.py:407
  9.4 2.5 %collective-permute-done = bf16[288,128]{1,0:T(8,128)(2,1)S(1)} collective-permute-done((bf16[288,128]{1,0:T(8,128)(2,1)}, bf16[288,128]{1,0:T(8,128)(2,1)S(1)}, u32[]{:S(2)}, u32[]{:S(2)}) %collective-permute-start) | collective-permute-done | bytes 73760 | tf_op jit(solution)/shard_map/ppermute | solution.py:406
  12.9 1.7 %collective-permute-start.3 = (bf16[864,128]{1,0:T(8,128)(2,1)S(1)}, bf16[864,128]{1,0:T(8,128)(2,1)S(1)}, u32[]{:S(2)}, u32[]{:S(2)}) collective-permute-start(bf16[864,128]{1,0:T(8,128)(2,1)S(1)} %constant_dynamic-update-slice_fusion.x_own), channel_id=1, source_target_pairs={{1,0},{2,1},{3,2},{4,3},{5,4},{6,5},{7,6},{8,7},{9,8},{10,9},{11,1... | collective-permute-start | bytes 663560 | tf_op jit(solution)/shard_map/ppermute | solution.py:407
  14.6 2.2 %shard_map.175 = (s32[128,128]{1,0:T(8,128)}, bf16[352,1024]{1,0:T(8,128)(2,1)}, f32[16,512]{1,0:T(8,128)}, f32[16,384]{1,0:T(8,128)}) custom-call(s32[32,512]{1,0:T(8,128)} %neighbours.1, s32[32,512]{1,0:T(8,128)} %mask.1, f32[3,512]{1,0:T(4,128)} %frac.5, s32[3,32]{1,0:T(4,128)} %waves.1), custom_call_target="tpu_custom_call" | custom-call | flops 2000000000 | bytes 4000000 | tf_op jit(solution)/shard_map/pallas_call | solution.py:441
  16.8 2.1 %collective-permute-done.3.x_high = bf16[864,128]{1,0:T(8,128)(2,1)S(1)} collective-permute-done((bf16[864,128]{1,0:T(8,128)(2,1)S(1)}, bf16[864,128]{1,0:T(8,128)(2,1)S(1)}, u32[]{:S(2)}, u32[]{:S(2)}) %collective-permute-start.3) | collective-permute-done | bytes 221216 | tf_op jit(solution)/shard_map/ppermute | solution.py:407
  18.9 3.4 %collective-permute-done.2.x_low = bf16[864,128]{1,0:T(8,128)(2,1)S(1)} collective-permute-done((bf16[864,128]{1,0:T(8,128)(2,1)S(1)}, bf16[864,128]{1,0:T(8,128)(2,1)S(1)}, u32[]{:S(2)}, u32[]{:S(2)}) %collective-permute-start.2) | collective-permute-done | bytes 221216 | tf_op jit(solution)/shard_map/ppermute | solution.py:406
  23.0 19.5 %shard_map.177 = (bf16[512,128]{1,0:T(8,128)(2,1)}, bf16[512,128]{1,0:T(8,128)(2,1)}, bf16[256,128]{1,0:T(8,128)(2,1)}, f32[128,128]{1,0:T(8,128)}) custom-call(s32[16384]{0:T(1024)} %bitcast.7, s32[256]{0:T(256)} %send.3, s32[128,128]{1,0:T(8,128)} %get-tuple-element.18.slots, f32[3,512]{1,0:T(4,128)} %frac.5, bf16[864,128]{1,0:T(8,128)(2,1)} %copy-done.7, ...), custom_call_target="tpu_custom_call" | custom-call | flops 4000000000 | bytes 4000000 | tf_op jit(solution)/shard_map/pallas_call | solution.py:447
  42.5 3.4 %collective-permute-start.4 = (bf16[256,128]{1,0:T(8,128)(2,1)}, bf16[256,128]{1,0:T(8,128)(2,1)S(1)}, u32[]{:S(2)}, u32[]{:S(2)}) collective-permute-start(bf16[256,128]{1,0:T(8,128)(2,1)} %get-tuple-element.22), channel_id=1, source_target_pairs={{0,16},{16,32},{32,48},{48,64},{64,80},{80,96},{96,112},{112,0},{1... | collective-permute-start | bytes 196616 | tf_op jit(solution)/shard_map/ppermute | solution.py:406
  45.8 2.3 %collective-permute-start.5 = (bf16[256,128]{1,0:T(8,128)(2,1)}, bf16[256,128]{1,0:T(8,128)(2,1)S(1)}, u32[]{:S(2)}, u32[]{:S(2)}) collective-permute-start(bf16[256,128]{1,0:T(8,128)(2,1)} %get-tuple-element.22), channel_id=1, source_target_pairs={{16,0},{32,16},{48,32},{64,48},{80,64},{96,80},{112,96},{0,112},{1... | collective-permute-start | bytes 196616 | tf_op jit(solution)/shard_map/ppermute | solution.py:407
  48.1 2.4 %collective-permute-done.4 = bf16[256,128]{1,0:T(8,128)(2,1)S(1)} collective-permute-done((bf16[256,128]{1,0:T(8,128)(2,1)}, bf16[256,128]{1,0:T(8,128)(2,1)S(1)}, u32[]{:S(2)}, u32[]{:S(2)}) %collective-permute-start.4) | collective-permute-done | bytes 65568 | tf_op jit(solution)/shard_map/ppermute | solution.py:406
  52.4 6.6 %shard_map.178.filters = bf16[8,2,512,256]{3,2,1,0:T(8,128)(2,1)} custom-call(f32[128,128]{1,0:T(8,128)} %get-tuple-element.21.chord, bf16[2,32,128]{2,1,0:T(8,128)(2,1)} %w1.3, bf16[2,128,128]{2,1,0:T(8,128)(2,1)} %w2.3), custom_call_target="tpu_custom_call" | custom-call | flops 4000000000 | bytes 8000000 | tf_op jit(solution)/shard_map/pallas_call | solution.py:463
  59.9 13.4 %shard_map.179 = (bf16[512,128]{1,0:T(8,128)(2,1)}, bf16[64,384]{1,0:T(8,128)(2,1)}, bf16[64,384]{1,0:T(8,128)(2,1)}) custom-call(s32[16384]{0:T(1024)} %bitcast.8, s32[1]{0:T(128)} %bitcast.1.core, bf16[8,2,512,256]{3,2,1,0:T(8,128)(2,1)} %shard_map.178.filters, bf16[768,128]{1,0:T(8,128)(2,1)} %copy-done.2, bf16[768,128]{1,0:T(8,128)(2,1)} %copy-done, ...), custom_call_target="tpu_custom_call" | custom-call | flops 1000000000 | bytes 8000000 | tf_op jit(solution)/shard_map/pallas_call | solution.py:474
  73.3 1.4 %collective-permute-done.8 = bf16[64,384]{1,0:T(8,128)(2,1)S(1)} collective-permute-done((bf16[64,384]{1,0:T(8,128)(2,1)}, bf16[64,384]{1,0:T(8,128)(2,1)S(1)}, u32[]{:S(2)}, u32[]{:S(2)}) %collective-permute-start.8) | collective-permute-done | bytes 49184 | tf_op jit(solution)/shard_map/ppermute | solution.py:418
  75.6 1.3 %collective-permute-start.11 = (bf16[64,384]{1,0:T(8,128)(2,1)S(1)}, bf16[64,384]{1,0:T(8,128)(2,1)S(1)}, u32[]{:S(2)}, u32[]{:S(2)}) collective-permute-start(bf16[64,384]{1,0:T(8,128)(2,1)S(1)} %add_convert_fusion.3), channel_id=1, source_target_pairs={{0,18},{1,19},{2,16},{3,17},{4,22},{5,23},{6,20},{7,21},{8,26},{9,... | collective-permute-start | bytes 147464 | tf_op jit(solution)/shard_map/ppermute | solution.py:418
  78.0 1.8 %collective-permute-start.9 = (bf16[64,384]{1,0:T(8,128)(2,1)S(1)}, bf16[64,384]{1,0:T(8,128)(2,1)S(1)}, u32[]{:S(2)}, u32[]{:S(2)}) collective-permute-start(bf16[64,384]{1,0:T(8,128)(2,1)S(1)} %add_convert_fusion.3), channel_id=1, source_target_pairs={{0,2},{1,3},{2,0},{3,1},{4,6},{5,7},{6,4},{7,5},{8,10},{9,11},{10,... | collective-permute-start | bytes 147464 | tf_op jit(solution)/shard_map/ppermute | solution.py:418
  81.0 1.9 %collective-permute-done.10 = bf16[64,384]{1,0:T(8,128)(2,1)S(1)} collective-permute-done((bf16[64,384]{1,0:T(8,128)(2,1)S(1)}, bf16[64,384]{1,0:T(8,128)(2,1)S(1)}, u32[]{:S(2)}, u32[]{:S(2)}) %collective-permute-start.10) | collective-permute-done | bytes 49184 | tf_op jit(solution)/shard_map/ppermute | solution.py:418
  82.9 3.4 %collective-permute-start.14 = (bf16[64,384]{1,0:T(8,128)(2,1)S(1)}, bf16[64,384]{1,0:T(8,128)(2,1)S(1)}, u32[]{:S(2)}, u32[]{:S(2)}) collective-permute-start(bf16[64,384]{1,0:T(8,128)(2,1)S(1)} %add_convert_fusion.2), channel_id=1, source_target_pairs={{0,12},{1,13},{2,14},{3,15},{4,8},{5,9},{6,10},{7,11},{8,4},{9,5},... | collective-permute-start | bytes 147464 | tf_op jit(solution)/shard_map/ppermute | solution.py:418
  88.3 3.5 %collective-permute-done.13 = bf16[64,384]{1,0:T(8,128)(2,1)S(1)} collective-permute-done((bf16[64,384]{1,0:T(8,128)(2,1)S(1)}, bf16[64,384]{1,0:T(8,128)(2,1)S(1)}, u32[]{:S(2)}, u32[]{:S(2)}) %collective-permute-start.13) | collective-permute-done | bytes 49184 | tf_op jit(solution)/shard_map/ppermute | solution.py:418
  91.9 2.8 %collective-permute-start.17 = (bf16[64,384]{1,0:T(8,128)(2,1)S(1)}, bf16[64,384]{1,0:T(8,128)(2,1)S(1)}, u32[]{:S(2)}, u32[]{:S(2)}) collective-permute-start(bf16[64,384]{1,0:T(8,128)(2,1)S(1)} %add_convert_fusion.1), channel_id=1, source_target_pairs={{0,96},{1,97},{2,98},{3,99},{4,100},{5,101},{6,102},{7,103},{8,104... | collective-permute-start | bytes 147464 | tf_op jit(solution)/shard_map/ppermute | solution.py:418
  97.3 3.1 %collective-permute-done.16 = bf16[64,384]{1,0:T(8,128)(2,1)S(1)} collective-permute-done((bf16[64,384]{1,0:T(8,128)(2,1)S(1)}, bf16[64,384]{1,0:T(8,128)(2,1)S(1)}, u32[]{:S(2)}, u32[]{:S(2)}) %collective-permute-start.16) | collective-permute-done | bytes 49184 | tf_op jit(solution)/shard_map/ppermute | solution.py:418
  100.5 1.2 %collective-permute-done.18.other_half = bf16[64,384]{1,0:T(8,128)(2,1)S(1)} collective-permute-done((bf16[64,384]{1,0:T(8,128)(2,1)S(1)}, bf16[64,384]{1,0:T(8,128)(2,1)S(1)}, u32[]{:S(2)}, u32[]{:S(2)}) %collective-permute-start.18) | collective-permute-done | bytes 49184 | tf_op jit(solution)/shard_map/ppermute | solution.py:418
  102.3 2.7 %shard_map.180 = (f32[16,512]{1,0:T(8,128)}, f32[1,512]{1,0:T(1,128)}) custom-call(s32[1]{0:T(128)} %bitcast.1.core, bf16[64,384]{1,0:T(8,128)(2,1)} %copy-done.3, bf16[64,384]{1,0:T(8,128)(2,1)} %copy-done.4, bf16[352,1024]{1,0:T(8,128)(2,1)} %get-tuple-element.25.phase, f32[16,512]{1,0:T(8,128)} %get-tuple-element.26.axis, f32[1,16]{1,0:T(1,128)} %bitcast.11, ...), custom_call_target="tpu_custom_call" | custom-call | flops 100000000 | bytes 2000000 | tf_op jit(solution)/shard_map/pallas_call | solution.py:486
  (46 shorter events, 12.8 us)
Async XLA Ops:
  2.8 9.1 %collective-permute-start = (bf16[288,128]{1,0:T(8,128)(2,1)}, bf16[288,128]{1,0:T(8,128)(2,1)S(1)}, u32[]{:S(2)}, u32[]{:S(2)}) collective-permute-start(bf16[288,128]{1,0:T(8,128)(2,1)} %get-tuple-element.19), channel_id=1, source_target_pairs={{0,16},{16,32},{32,48},{48,64},{64,80},{80,96},{96,112},{112,0},{1... | collective-permute-start | bytes 221192 | tf_op jit(solution)/shard_map/ppermute | solution.py:406
  5.9 6.9 %collective-permute-start.1 = (bf16[288,128]{1,0:T(8,128)(2,1)}, bf16[288,128]{1,0:T(8,128)(2,1)S(1)}, u32[]{:S(2)}, u32[]{:S(2)}) collective-permute-start(bf16[288,128]{1,0:T(8,128)(2,1)} %get-tuple-element.19), channel_id=1, source_target_pairs={{16,0},{32,16},{48,32},{64,48},{80,64},{96,80},{112,96},{0,112},{1... | collective-permute-start | bytes 221192 | tf_op jit(solution)/shard_map/ppermute | solution.py:407
  12.9 9.4 %copy-start.5 = (bf16[864,128]{1,0:T(8,128)(2,1)}, bf16[864,128]{1,0:T(8,128)(2,1)S(1)}, u32[]{:S(2)}) copy-start(bf16[864,128]{1,0:T(8,128)(2,1)S(1)} %constant_dynamic-update-slice_fusion.x_own) | copy-start | bytes 663556
  12.9 6.0 %collective-permute-start.3 = (bf16[864,128]{1,0:T(8,128)(2,1)S(1)}, bf16[864,128]{1,0:T(8,128)(2,1)S(1)}, u32[]{:S(2)}, u32[]{:S(2)}) collective-permute-start(bf16[864,128]{1,0:T(8,128)(2,1)S(1)} %constant_dynamic-update-slice_fusion.x_own), channel_id=1, source_target_pairs={{1,0},{2,1},{3,2},{4,3},{5,4},{6,5},{7,6},{8,7},{9,8},{10,9},{11,1... | collective-permute-start | bytes 663560 | tf_op jit(solution)/shard_map/ppermute | solution.py:407
  14.6 7.7 %collective-permute-start.2 = (bf16[864,128]{1,0:T(8,128)(2,1)S(1)}, bf16[864,128]{1,0:T(8,128)(2,1)S(1)}, u32[]{:S(2)}, u32[]{:S(2)}) collective-permute-start(bf16[864,128]{1,0:T(8,128)(2,1)S(1)} %constant_dynamic-update-slice_fusion.x_own), channel_id=1, source_target_pairs={{0,1},{1,2},{2,3},{3,4},{4,5},{5,6},{6,7},{7,8},{8,9},{9,10},{10,1... | collective-permute-start | bytes 663560 | tf_op jit(solution)/shard_map/ppermute | solution.py:406
  18.9 3.4 %copy-start.6 = (bf16[864,128]{1,0:T(8,128)(2,1)}, bf16[864,128]{1,0:T(8,128)(2,1)S(1)}, u32[]{:S(2)}) copy-start(bf16[864,128]{1,0:T(8,128)(2,1)S(1)} %collective-permute-done.3.x_high) | copy-start | bytes 663556
  42.5 8.1 %collective-permute-start.4 = (bf16[256,128]{1,0:T(8,128)(2,1)}, bf16[256,128]{1,0:T(8,128)(2,1)S(1)}, u32[]{:S(2)}, u32[]{:S(2)}) collective-permute-start(bf16[256,128]{1,0:T(8,128)(2,1)} %get-tuple-element.22), channel_id=1, source_target_pairs={{0,16},{16,32},{32,48},{48,64},{64,80},{80,96},{96,112},{112,0},{1... | collective-permute-start | bytes 196616 | tf_op jit(solution)/shard_map/ppermute | solution.py:406
  45.8 6.0 %collective-permute-start.5 = (bf16[256,128]{1,0:T(8,128)(2,1)}, bf16[256,128]{1,0:T(8,128)(2,1)S(1)}, u32[]{:S(2)}, u32[]{:S(2)}) collective-permute-start(bf16[256,128]{1,0:T(8,128)(2,1)} %get-tuple-element.22), channel_id=1, source_target_pairs={{16,0},{32,16},{48,32},{64,48},{80,64},{96,80},{112,96},{0,112},{1... | collective-permute-start | bytes 196616 | tf_op jit(solution)/shard_map/ppermute | solution.py:407
  51.8 7.2 %copy-start = (bf16[768,128]{1,0:T(8,128)(2,1)}, bf16[768,128]{1,0:T(8,128)(2,1)S(1)}, u32[]{:S(2)}) copy-start(bf16[768,128]{1,0:T(8,128)(2,1)S(1)} %constant_dynamic-update-slice_fusion.3.x_own) | copy-start | bytes 589828
  51.8 7.2 %collective-permute-start.7 = (bf16[768,128]{1,0:T(8,128)(2,1)S(1)}, bf16[768,128]{1,0:T(8,128)(2,1)S(1)}, u32[]{:S(2)}, u32[]{:S(2)}) collective-permute-start(bf16[768,128]{1,0:T(8,128)(2,1)S(1)} %constant_dynamic-update-slice_fusion.3.x_own), channel_id=1, source_target_pairs={{1,0},{2,1},{3,2},{4,3},{5,4},{6,5},{7,6},{8,7},{9,8},{10,9},{11,1... | collective-permute-start | bytes 589832 | tf_op jit(solution)/shard_map/ppermute | solution.py:407
  51.9 7.3 %collective-permute-start.6 = (bf16[768,128]{1,0:T(8,128)(2,1)S(1)}, bf16[768,128]{1,0:T(8,128)(2,1)S(1)}, u32[]{:S(2)}, u32[]{:S(2)}) collective-permute-start(bf16[768,128]{1,0:T(8,128)(2,1)S(1)} %constant_dynamic-update-slice_fusion.3.x_own), channel_id=1, source_target_pairs={{0,1},{1,2},{2,3},{3,4},{4,5},{5,6},{6,7},{7,8},{8,9},{9,10},{10,1... | collective-permute-start | bytes 589832 | tf_op jit(solution)/shard_map/ppermute | solution.py:406
  59.0 0.7 copy-start.1
  73.3 1.4 %collective-permute-start.8 = (bf16[64,384]{1,0:T(8,128)(2,1)}, bf16[64,384]{1,0:T(8,128)(2,1)S(1)}, u32[]{:S(2)}, u32[]{:S(2)}) collective-permute-start(bf16[64,384]{1,0:T(8,128)(2,1)} %get-tuple-element.30), channel_id=1, source_target_pairs={{0,1},{1,0},{2,3},{3,2},{4,5},{5,4},{6,7},{7,6},{8,9},{9,8},{10,11... | collective-permute-start | bytes 147464 | tf_op jit(solution)/shard_map/ppermute | solution.py:418
  75.6 5.4 %collective-permute-start.11 = (bf16[64,384]{1,0:T(8,128)(2,1)S(1)}, bf16[64,384]{1,0:T(8,128)(2,1)S(1)}, u32[]{:S(2)}, u32[]{:S(2)}) collective-permute-start(bf16[64,384]{1,0:T(8,128)(2,1)S(1)} %add_convert_fusion.3), channel_id=1, source_target_pairs={{0,18},{1,19},{2,16},{3,17},{4,22},{5,23},{6,20},{7,21},{8,26},{9,... | collective-permute-start | bytes 147464 | tf_op jit(solution)/shard_map/ppermute | solution.py:418
  76.9 5.9 %collective-permute-start.10 = (bf16[64,384]{1,0:T(8,128)(2,1)S(1)}, bf16[64,384]{1,0:T(8,128)(2,1)S(1)}, u32[]{:S(2)}, u32[]{:S(2)}) collective-permute-start(bf16[64,384]{1,0:T(8,128)(2,1)S(1)} %add_convert_fusion.3), channel_id=1, source_target_pairs={{0,16},{1,17},{2,18},{3,19},{4,20},{5,21},{6,22},{7,23},{8,24},{9,... | collective-permute-start | bytes 147464 | tf_op jit(solution)/shard_map/ppermute | solution.py:418
  78.0 4.9 %collective-permute-start.9 = (bf16[64,384]{1,0:T(8,128)(2,1)S(1)}, bf16[64,384]{1,0:T(8,128)(2,1)S(1)}, u32[]{:S(2)}, u32[]{:S(2)}) collective-permute-start(bf16[64,384]{1,0:T(8,128)(2,1)S(1)} %add_convert_fusion.3), channel_id=1, source_target_pairs={{0,2},{1,3},{2,0},{3,1},{4,6},{5,7},{6,4},{7,5},{8,10},{9,11},{10,... | collective-permute-start | bytes 147464 | tf_op jit(solution)/shard_map/ppermute | solution.py:418
  82.9 5.4 %collective-permute-start.14 = (bf16[64,384]{1,0:T(8,128)(2,1)S(1)}, bf16[64,384]{1,0:T(8,128)(2,1)S(1)}, u32[]{:S(2)}, u32[]{:S(2)}) collective-permute-start(bf16[64,384]{1,0:T(8,128)(2,1)S(1)} %add_convert_fusion.2), channel_id=1, source_target_pairs={{0,12},{1,13},{2,14},{3,15},{4,8},{5,9},{6,10},{7,11},{8,4},{9,5},... | collective-permute-start | bytes 147464 | tf_op jit(solution)/shard_map/ppermute | solution.py:418
  86.2 5.6 %collective-permute-start.13 = (bf16[64,384]{1,0:T(8,128)(2,1)S(1)}, bf16[64,384]{1,0:T(8,128)(2,1)S(1)}, u32[]{:S(2)}, u32[]{:S(2)}) collective-permute-start(bf16[64,384]{1,0:T(8,128)(2,1)S(1)} %add_convert_fusion.2), channel_id=1, source_target_pairs={{0,8},{1,9},{2,10},{3,11},{4,12},{5,13},{6,14},{7,15},{8,0},{9,1},... | collective-permute-start | bytes 147464 | tf_op jit(solution)/shard_map/ppermute | solution.py:418
  86.3 5.6 %collective-permute-start.12 = (bf16[64,384]{1,0:T(8,128)(2,1)S(1)}, bf16[64,384]{1,0:T(8,128)(2,1)S(1)}, u32[]{:S(2)}, u32[]{:S(2)}) collective-permute-start(bf16[64,384]{1,0:T(8,128)(2,1)S(1)} %add_convert_fusion.2), channel_id=1, source_target_pairs={{0,4},{1,5},{2,6},{3,7},{4,0},{5,1},{6,2},{7,3},{8,12},{9,13},{10,... | collective-permute-start | bytes 147464 | tf_op jit(solution)/shard_map/ppermute | solution.py:418
  91.9 5.4 %collective-permute-start.17 = (bf16[64,384]{1,0:T(8,128)(2,1)S(1)}, bf16[64,384]{1,0:T(8,128)(2,1)S(1)}, u32[]{:S(2)}, u32[]{:S(2)}) collective-permute-start(bf16[64,384]{1,0:T(8,128)(2,1)S(1)} %add_convert_fusion.1), channel_id=1, source_target_pairs={{0,96},{1,97},{2,98},{3,99},{4,100},{5,101},{6,102},{7,103},{8,104... | collective-permute-start | bytes 147464 | tf_op jit(solution)/shard_map/ppermute | solution.py:418
  94.7 5.6 %collective-permute-start.16 = (bf16[64,384]{1,0:T(8,128)(2,1)S(1)}, bf16[64,384]{1,0:T(8,128)(2,1)S(1)}, u32[]{:S(2)}, u32[]{:S(2)}) collective-permute-start(bf16[64,384]{1,0:T(8,128)(2,1)S(1)} %add_convert_fusion.1), channel_id=1, source_target_pairs={{0,64},{1,65},{2,66},{3,67},{4,68},{5,69},{6,70},{7,71},{8,72},{9,... | collective-permute-start | bytes 147464 | tf_op jit(solution)/shard_map/ppermute | solution.py:418
  95.7 4.7 %collective-permute-start.15 = (bf16[64,384]{1,0:T(8,128)(2,1)S(1)}, bf16[64,384]{1,0:T(8,128)(2,1)S(1)}, u32[]{:S(2)}, u32[]{:S(2)}) collective-permute-start(bf16[64,384]{1,0:T(8,128)(2,1)S(1)} %add_convert_fusion.1), channel_id=1, source_target_pairs={{0,32},{1,33},{2,34},{3,35},{4,36},{5,37},{6,38},{7,39},{8,40},{9,... | collective-permute-start | bytes 147464 | tf_op jit(solution)/shard_map/ppermute | solution.py:418
  100.3 1.3 %copy-start.3 = (bf16[64,384]{1,0:T(8,128)(2,1)}, bf16[64,384]{1,0:T(8,128)(2,1)S(1)}, u32[]{:S(2)}) copy-start(bf16[64,384]{1,0:T(8,128)(2,1)S(1)} %add_convert_fusion.own_half) | copy-start | bytes 147460
  100.4 1.3 %collective-permute-start.18 = (bf16[64,384]{1,0:T(8,128)(2,1)S(1)}, bf16[64,384]{1,0:T(8,128)(2,1)S(1)}, u32[]{:S(2)}, u32[]{:S(2)}) collective-permute-start(bf16[64,384]{1,0:T(8,128)(2,1)S(1)} %add_convert_fusion.own_half), channel_id=1, source_target_pairs={{0,1},{1,0},{2,3},{3,2},{4,5},{5,4},{6,7},{7,6},{8,9},{9,8},{10,11... | collective-permute-start | bytes 147464 | tf_op jit(solution)/shard_map/ppermute | solution.py:418
  (3 other events, 2.0 us)

commit v3 on v2

--- a/solution.py
+++ b/solution.py
@@ -263,11 +263,13 @@
 
 
 def layer_kernel(
-    slots_s, send, slots, frac, x_low, x_own, x_high, projected, state,
+    slots_hbm, send, slots, frac, x_low, x_own, x_high, projected, state,
     w1, w2, w_update1, w_update2, w_in,
     state_out, proj_out, send_out, chord_out,
-    table, places, wide1, wide2, filters, total, proj_table,
+    table, places, wide1, wide2, filters, total, proj_table, slots_s, arrived,
 ):
+    fetch = pltpu.make_async_copy(slots_hbm, slots_s, arrived)
+    fetch.start()
     rows_in = (x_low, x_own, x_high)
     fill_table(table, projected, rows_in, PACK)
     fill_filter_weights(w1, w2, 0, wide1, wide2)
@@ -283,6 +285,7 @@
         return carry
 
     lax.fori_loop(0, 8, make, 0)
+    fetch.wait()
     lax.fori_loop(0, 32, use, 0)
     new_state = update_tail(total, state, w_update1, w_update2, 0)
     state_out[...] = new_state
@@ -342,7 +345,7 @@
 
 
 def field_kernel(
-    core, own_half, other_half, phase, axis, screening, state, w_head, w_potential, w_energy,
+    core, own_half, other_half, phase, axis, screening, head, w_potential, w_energy,
     potentials_out, energies_out, response, sums,
 ):
     mine = pl.multiple_of(core[0] * HALF, HALF)
@@ -374,7 +377,7 @@
         total = total + part[:, :T] * axis[n : n + 1, :] + part[:, T:] * axis[8 + n : 9 + n, :]
     potentials = total * (4.0 / 256.0)
     potentials_out[...] = potentials
-    summed = dot(state[...], w_head[...]) + dot(potentials.astype(bf16), w_potential[...], ((0,), (0,)))
+    summed = head[...] + dot(potentials.astype(bf16), w_potential[...], ((0,), (0,)))
     readout = silu(summed).astype(bf16)
     energies_out[...] = dot(w_energy[...], readout, ((1,), (1,)))
 
@@ -398,6 +401,10 @@
     )
 
 
+def near(x):
+    return pltpu.with_memory_space_constraint(x, pltpu.VMEM)
+
+
 def halo(block):
     for axis in ("gx", "yz"):
         count = lax.axis_size(axis)
@@ -407,7 +414,7 @@
         high = lax.ppermute(block, axis, backward)
         if axis == "gx":
             block = jnp.concatenate([low, block, high], axis=0)
-    return low, block, high
+    return near(low), near(block), near(high)
 
 
 RINGS = ((2, 16, 18), (4, 8, 12), (32, 64, 96))
@@ -445,17 +452,18 @@
     )(neighbours, nbr_mask, frac, wavevectors)
     x_low, x_own, x_high = halo(sent)
     state, projected, sent, chord = call(
-        layer_kernel, [SMEM, SMEM] + [VMEM] * 12,
+        layer_kernel, [pl.BlockSpec(memory_space=pl.ANY), SMEM] + [VMEM] * 12,
         (shape(T, C, dtype=bf16), shape(T, C, dtype=bf16), shape(H, C, dtype=bf16), shape(4 * K, 128)),
         [
             pltpu.VMEM((SLOTS + 8, C), f32), pltpu.VMEM((72, 128), f32),
             pltpu.VMEM((4 * NR, 4 * C), bf16), pltpu.VMEM((2 * C, 2 * C), bf16),
             pltpu.VMEM((8, 2, T, 2 * C), bf16),
             pltpu.VMEM((T, C), f32), pltpu.VMEM((T, C), f32),
+            pltpu.SMEM((K * T,), i32), pltpu.SemaphoreType.DMA,
         ], 4_000_000_000, 4_000_000,
     )(
-        slots.reshape(-1), send_list, slots, frac, x_low, x_own, x_high, projected, features,
-        w_filter1, w_filter2, w_update1, w_update2, w_in,
+        slots.reshape(-1), send_list, slots, near(frac), x_low, x_own, x_high, near(projected), near(features),
+        near(w_filter1), near(w_filter2), near(w_update1), near(w_update2), near(w_in),
     )
     x_low, x_own, x_high = halo(sent)
     whole = lambda a: pl.BlockSpec(a.shape, lambda i: (0,) * a.ndim)
@@ -467,7 +475,9 @@
         scratch_shapes=[pltpu.VMEM((4 * NR, 4 * C), bf16), pltpu.VMEM((2 * C, 2 * C), bf16)],
         cost_estimate=pl.CostEstimate(flops=4_000_000_000, bytes_accessed=8_000_000, transcendentals=0),
     )(chord, w_filter1, w_filter2)
-    rest = (x_low, x_own, x_high, projected, state, w_update1, w_update2, w_charge.T, phase, axis, digits)
+    phase, axis = near(phase), near(axis)
+    rest = (x_low, x_own, x_high, near(projected), near(state), near(w_update1), near(w_update2))
+    rest = rest + (near(w_charge.T), phase, axis, near(digits))
     half = shape(HALF, SUM_LANES, dtype=bf16)
     half_spec = pl.BlockSpec(half.shape, lambda i: (0, 0))
     core = (lax.axis_index("yz") & 1).reshape(1)
@@ -483,12 +493,13 @@
         cost_estimate=pl.CostEstimate(flops=1_000_000_000, bytes_accessed=8_000_000, transcendentals=0),
     )(slots.reshape(-1), core, filters, *rest)
     own_half, other_half = sum_everywhere(keep, give)
+    head = dot(embeddings, w_head)
     potentials, energies = call(
-        field_kernel, [SMEM] + [VMEM] * 9, (shape(Q, T), shape(1, T)),
+        field_kernel, [SMEM] + [VMEM] * 8, (shape(Q, T), shape(1, T)),
         [pltpu.VMEM((ROWS, 2 * BETA), bf16), pltpu.VMEM((SUM_ROWS, SUM_LANES), f32)], 100_000_000, 2_000_000,
     )(
-        core, own_half, other_half, phase, axis, screening.reshape(1, Q), embeddings, w_head, w_potential,
-        w_energy.reshape(1, C),
+        core, near(own_half), near(other_half), phase, axis, near(screening.reshape(1, Q)), near(head),
+        near(w_potential), near(w_energy.reshape(1, C)),
     )
     return embeddings, potentials, energies.reshape(T)
 

time: 106 us -> 103 us (0.972)
  Pallas kernels: 46.6 us -> 44.4 us
  local copies, waits for them, and re-layouts: 3.78 us -> 1.87 us
  waiting for transfers between devices: 25.7 us -> 24.6 us
  matrix products: 0 us -> 1.07 us
    pallas_call x2, Pallas kernels: 22.1 us -> 19.7 us  [the longest x1 18.4 us: shards(): call(layer_kernel, [pl.BlockSpec(memory_space=pl.ANY), SMEM] + [VMEM] * 1...]
    unnamed x20 -> x40, local copies, waits for them, and re-layouts: 3.76 us -> 1.84 us
    dot_general x0 -> x1, matrix products: none -> 1.07 us  [dot(): return lax.dot_general(a, b, (dims, ((), ())), preferred_element_type=f32)]
  transfers between devices with their start and end apart: 19 -> 19, of which waited for: 14 -> 13; matrix products, arithmetic and copies ran while one was open for 2% -> 3% of each run, Pallas kernels for 8% -> 9%
where the time goes in v3:
time: 103 us; the launch traced here: 101 us
  Pallas kernels  44.4 us (43%)
  starting transfers between devices  27.3 us (27%)
  waiting for transfers between devices  24.6 us (24%)
  local copies, waits for them, and re-layouts  1.87 us (2%)
  matrix products  1.07 us (1%)
    pallas_call x1, Pallas kernels, shards(): call(layer_kernel, [pl.BlockSpec(memory_space=pl.ANY), SMEM] + [VMEM] * 1...  18.4 us
    ppermute x11, waiting for transfers between devices, exchange(): lax.ppermute(part, ('gx', 'yz'), [(i, i ^ offset) for i in range(count)])  13.7 us
    pallas_call x1, Pallas kernels, shards(): pl.pallas_call(last_layer_kernel, grid=(4,), out_shape=(shape(T, C, dtype...  13.4 us
    ppermute x11, starting transfers between devices, exchange(): lax.ppermute(part, ('gx', 'yz'), [(i, i ^ offset) for i in range(count)])  12.6 us
    ppermute x4, waiting for transfers between devices, halo(): low = lax.ppermute(block, axis, forward)  8.33 us
    ppermute x4, starting transfers between devices, halo(): high = lax.ppermute(block, axis, backward)  7.57 us
    ppermute x4, starting transfers between devices, halo(): low = lax.ppermute(block, axis, forward)  7.06 us
    pallas_call x1, Pallas kernels, shards(): pl.pallas_call(filter_kernel, grid=(4,), out_shape=shape(8, 2, T, 2 * C,...  6.75 us
  transfers between devices with their start and end apart: 19, of which 13 were waited for; matrix products, arithmetic and copies ran while one was open for 3% of the time, Pallas kernels for 9%

profile of v3, /device:TPU:0, one launch (start us, length us, event | category | flops | bytes accessed | tf_op | source)
XLA Modules:
  0.0 101.0 jit_solution(1381351295754335111)
XLA Ops:
  0.7 2.3 %shard_map.176 = (bf16[512,128]{1,0:T(8,128)(2,1)}, bf16[288,128]{1,0:T(8,128)(2,1)}) custom-call(s32[256]{0:T(256)} %send.3, s32[2,128]{1,0:T(2,128)} %bitcast.14, bf16[512,128]{1,0:T(8,128)(2,1)} %state.1, f32[3,512]{1,0:T(4,128)} %frac.5, bf16[2,128,128]{2,1,0:T(8,128)(2,1)} %w_in.3), custom_call_target="tpu_custom_call" | custom-call | flops 20000000 | bytes 300000 | tf_op jit(solution)/shard_map/pallas_call | solution.py:443
  3.0 3.1 %collective-permute-start = (bf16[288,128]{1,0:T(8,128)(2,1)}, bf16[288,128]{1,0:T(8,128)(2,1)S(1)}, u32[]{:S(2)}, u32[]{:S(2)}) collective-permute-start(bf16[288,128]{1,0:T(8,128)(2,1)} %get-tuple-element.19), channel_id=1, source_target_pairs={{0,16},{16,32},{32,48},{48,64},{64,80},{80,96},{96,112},{112,0},{1... | collective-permute-start | bytes 221192 | tf_op jit(solution)/shard_map/ppermute | solution.py:413
  6.1 3.5 %collective-permute-start.1 = (bf16[288,128]{1,0:T(8,128)(2,1)}, bf16[288,128]{1,0:T(8,128)(2,1)S(1)}, u32[]{:S(2)}, u32[]{:S(2)}) collective-permute-start(bf16[288,128]{1,0:T(8,128)(2,1)} %get-tuple-element.19), channel_id=1, source_target_pairs={{16,0},{32,16},{48,32},{64,48},{80,64},{96,80},{112,96},{0,112},{1... | collective-permute-start | bytes 221192 | tf_op jit(solution)/shard_map/ppermute | solution.py:414
  9.7 2.5 %collective-permute-done = bf16[288,128]{1,0:T(8,128)(2,1)S(1)} collective-permute-done((bf16[288,128]{1,0:T(8,128)(2,1)}, bf16[288,128]{1,0:T(8,128)(2,1)S(1)}, u32[]{:S(2)}, u32[]{:S(2)}) %collective-permute-start) | collective-permute-done | bytes 73760 | tf_op jit(solution)/shard_map/ppermute | solution.py:413
  13.1 1.7 %collective-permute-start.3 = (bf16[864,128]{1,0:T(8,128)(2,1)S(1)}, bf16[864,128]{1,0:T(8,128)(2,1)S(1)}, u32[]{:S(2)}, u32[]{:S(2)}) collective-permute-start(bf16[864,128]{1,0:T(8,128)(2,1)S(1)} %constant_dynamic-update-slice_fusion.x_own), channel_id=1, source_target_pairs={{1,0},{2,1},{3,2},{4,3},{5,4},{6,5},{7,6},{8,7},{9,8},{10,9},{11,1... | collective-permute-start | bytes 663560 | tf_op jit(solution)/shard_map/ppermute | solution.py:414
  14.8 2.2 %shard_map.175 = (s32[128,128]{1,0:T(8,128)}, bf16[352,1024]{1,0:T(8,128)(2,1)}, f32[16,512]{1,0:T(8,128)}, f32[16,384]{1,0:T(8,128)}) custom-call(s32[32,512]{1,0:T(8,128)} %neighbours.1, s32[32,512]{1,0:T(8,128)} %mask.1, f32[3,512]{1,0:T(4,128)} %frac.5, s32[3,32]{1,0:T(4,128)} %waves.1), custom_call_target="tpu_custom_call" | custom-call | flops 2000000000 | bytes 4000000 | tf_op jit(solution)/shard_map/pallas_call | solution.py:448
  17.0 2.1 %collective-permute-done.3.x_high = bf16[864,128]{1,0:T(8,128)(2,1)S(1)} collective-permute-done((bf16[864,128]{1,0:T(8,128)(2,1)S(1)}, bf16[864,128]{1,0:T(8,128)(2,1)S(1)}, u32[]{:S(2)}, u32[]{:S(2)}) %collective-permute-start.3) | collective-permute-done | bytes 221216 | tf_op jit(solution)/shard_map/ppermute | solution.py:414
  19.1 3.4 %collective-permute-done.2.x_low = bf16[864,128]{1,0:T(8,128)(2,1)S(1)} collective-permute-done((bf16[864,128]{1,0:T(8,128)(2,1)S(1)}, bf16[864,128]{1,0:T(8,128)(2,1)S(1)}, u32[]{:S(2)}, u32[]{:S(2)}) %collective-permute-start.2) | collective-permute-done | bytes 221216 | tf_op jit(solution)/shard_map/ppermute | solution.py:413
  22.6 18.4 %shard_map.177 = (bf16[512,128]{1,0:T(8,128)(2,1)}, bf16[512,128]{1,0:T(8,128)(2,1)}, bf16[256,128]{1,0:T(8,128)(2,1)}, f32[128,128]{1,0:T(8,128)}) custom-call(s32[16384]{0:T(1024)} %bitcast.12, s32[256]{0:T(256)} %send.3, s32[128,128]{1,0:T(8,128)} %get-tuple-element.18.slots, f32[3,512]{1,0:T(4,128)S(1)} %copy-done.10, ...), custom_call_target="tpu_custom_call" | custom-call | flops 4000000000 | bytes 4000000 | tf_op jit(solution)/shard_map/pallas_call | solution.py:454
  41.0 3.4 %collective-permute-start.4 = (bf16[256,128]{1,0:T(8,128)(2,1)}, bf16[256,128]{1,0:T(8,128)(2,1)S(1)}, u32[]{:S(2)}, u32[]{:S(2)}) collective-permute-start(bf16[256,128]{1,0:T(8,128)(2,1)} %get-tuple-element.22), channel_id=1, source_target_pairs={{0,16},{16,32},{32,48},{48,64},{64,80},{80,96},{96,112},{112,0},{1... | collective-permute-start | bytes 196616 | tf_op jit(solution)/shard_map/ppermute | solution.py:413
  44.4 2.3 %collective-permute-start.5 = (bf16[256,128]{1,0:T(8,128)(2,1)}, bf16[256,128]{1,0:T(8,128)(2,1)S(1)}, u32[]{:S(2)}, u32[]{:S(2)}) collective-permute-start(bf16[256,128]{1,0:T(8,128)(2,1)} %get-tuple-element.22), channel_id=1, source_target_pairs={{16,0},{32,16},{48,32},{64,48},{80,64},{96,80},{112,96},{0,112},{1... | collective-permute-start | bytes 196616 | tf_op jit(solution)/shard_map/ppermute | solution.py:414
  46.7 2.4 %collective-permute-done.4 = bf16[256,128]{1,0:T(8,128)(2,1)S(1)} collective-permute-done((bf16[256,128]{1,0:T(8,128)(2,1)}, bf16[256,128]{1,0:T(8,128)(2,1)S(1)}, u32[]{:S(2)}, u32[]{:S(2)}) %collective-permute-start.4) | collective-permute-done | bytes 65568 | tf_op jit(solution)/shard_map/ppermute | solution.py:413
  51.0 6.8 %shard_map.178.filters = bf16[8,2,512,256]{3,2,1,0:T(8,128)(2,1)} custom-call(f32[128,128]{1,0:T(8,128)} %get-tuple-element.21.chord, bf16[2,32,128]{2,1,0:T(8,128)(2,1)} %w1.3, bf16[2,128,128]{2,1,0:T(8,128)(2,1)} %w2.3), custom_call_target="tpu_custom_call" | custom-call | flops 4000000000 | bytes 8000000 | tf_op jit(solution)/shard_map/pallas_call | solution.py:471
  57.8 13.4 %shard_map.179 = (bf16[512,128]{1,0:T(8,128)(2,1)}, bf16[64,384]{1,0:T(8,128)(2,1)}, bf16[64,384]{1,0:T(8,128)(2,1)}) custom-call(s32[16384]{0:T(1024)} %bitcast.13, s32[1]{0:T(128)} %bitcast.1.core, bf16[8,2,512,256]{3,2,1,0:T(8,128)(2,1)} %shard_map.178.filters, bf16[768,128]{1,0:T(8,128)(2,1)S(1)} %collective-permute-done.6.x_low, ...), custom_call_target="tpu_custom_call" | custom-call | flops 1000000000 | bytes 8000000 | tf_op jit(solution)/shard_map/pallas_call | solution.py:484
  71.3 1.4 %collective-permute-done.8 = bf16[64,384]{1,0:T(8,128)(2,1)S(1)} collective-permute-done((bf16[64,384]{1,0:T(8,128)(2,1)}, bf16[64,384]{1,0:T(8,128)(2,1)S(1)}, u32[]{:S(2)}, u32[]{:S(2)}) %collective-permute-start.8) | collective-permute-done | bytes 49184 | tf_op jit(solution)/shard_map/ppermute | solution.py:425
  73.5 1.4 %collective-permute-start.11 = (bf16[64,384]{1,0:T(8,128)(2,1)S(1)}, bf16[64,384]{1,0:T(8,128)(2,1)S(1)}, u32[]{:S(2)}, u32[]{:S(2)}) collective-permute-start(bf16[64,384]{1,0:T(8,128)(2,1)S(1)} %add_convert_fusion.3), channel_id=1, source_target_pairs={{0,18},{1,19},{2,16},{3,17},{4,22},{5,23},{6,20},{7,21},{8,26},{9,... | collective-permute-start | bytes 147464 | tf_op jit(solution)/shard_map/ppermute | solution.py:425
  75.8 1.9 %collective-permute-start.9 = (bf16[64,384]{1,0:T(8,128)(2,1)S(1)}, bf16[64,384]{1,0:T(8,128)(2,1)S(1)}, u32[]{:S(2)}, u32[]{:S(2)}) collective-permute-start(bf16[64,384]{1,0:T(8,128)(2,1)S(1)} %add_convert_fusion.3), channel_id=1, source_target_pairs={{0,2},{1,3},{2,0},{3,1},{4,6},{5,7},{6,4},{7,5},{8,10},{9,11},{10,... | collective-permute-start | bytes 147464 | tf_op jit(solution)/shard_map/ppermute | solution.py:425
  78.9 2.1 %collective-permute-done.10 = bf16[64,384]{1,0:T(8,128)(2,1)S(1)} collective-permute-done((bf16[64,384]{1,0:T(8,128)(2,1)S(1)}, bf16[64,384]{1,0:T(8,128)(2,1)S(1)}, u32[]{:S(2)}, u32[]{:S(2)}) %collective-permute-start.10) | collective-permute-done | bytes 49184 | tf_op jit(solution)/shard_map/ppermute | solution.py:425
  81.0 3.2 %collective-permute-start.14 = (bf16[64,384]{1,0:T(8,128)(2,1)S(1)}, bf16[64,384]{1,0:T(8,128)(2,1)S(1)}, u32[]{:S(2)}, u32[]{:S(2)}) collective-permute-start(bf16[64,384]{1,0:T(8,128)(2,1)S(1)} %add_convert_fusion.2), channel_id=1, source_target_pairs={{0,12},{1,13},{2,14},{3,15},{4,8},{5,9},{6,10},{7,11},{8,4},{9,5},... | collective-permute-start | bytes 147464 | tf_op jit(solution)/shard_map/ppermute | solution.py:425
  85.2 1.2 %collective-permute-done.14 = bf16[64,384]{1,0:T(8,128)(2,1)S(1)} collective-permute-done((bf16[64,384]{1,0:T(8,128)(2,1)S(1)}, bf16[64,384]{1,0:T(8,128)(2,1)S(1)}, u32[]{:S(2)}, u32[]{:S(2)}) %collective-permute-start.14) | collective-permute-done | bytes 49184 | tf_op jit(solution)/shard_map/ppermute | solution.py:425
  86.4 3.4 %collective-permute-done.13 = bf16[64,384]{1,0:T(8,128)(2,1)S(1)} collective-permute-done((bf16[64,384]{1,0:T(8,128)(2,1)S(1)}, bf16[64,384]{1,0:T(8,128)(2,1)S(1)}, u32[]{:S(2)}, u32[]{:S(2)}) %collective-permute-start.13) | collective-permute-done | bytes 49184 | tf_op jit(solution)/shard_map/ppermute | solution.py:425
  89.8 2.9 %collective-permute-start.17 = (bf16[64,384]{1,0:T(8,128)(2,1)S(1)}, bf16[64,384]{1,0:T(8,128)(2,1)S(1)}, u32[]{:S(2)}, u32[]{:S(2)}) collective-permute-start(bf16[64,384]{1,0:T(8,128)(2,1)S(1)} %add_convert_fusion.1), channel_id=1, source_target_pairs={{0,96},{1,97},{2,98},{3,99},{4,100},{5,101},{6,102},{7,103},{8,104... | collective-permute-start | bytes 147464 | tf_op jit(solution)/shard_map/ppermute | solution.py:425
  95.2 3.1 %collective-permute-done.16 = bf16[64,384]{1,0:T(8,128)(2,1)S(1)} collective-permute-done((bf16[64,384]{1,0:T(8,128)(2,1)S(1)}, bf16[64,384]{1,0:T(8,128)(2,1)S(1)}, u32[]{:S(2)}, u32[]{:S(2)}) %collective-permute-start.16) | collective-permute-done | bytes 49184 | tf_op jit(solution)/shard_map/ppermute | solution.py:425
  99.6 1.3 %shard_map.180 = (f32[16,512]{1,0:T(8,128)}, f32[1,512]{1,0:T(1,128)}) custom-call(s32[1]{0:T(128)} %bitcast.1.core, bf16[64,384]{1,0:T(8,128)(2,1)S(1)} %add_convert_fusion.own_half, bf16[64,384]{1,0:T(8,128)(2,1)S(1)} %collective-permute-done.18.other_half, bf16[352,1024]{1,0:T(8,128)(2,1)S(1)} %copy-done.1, f32[16,512]{1,0:T(8,128)S(1)} %copy-done.2, ...), custom_call_target="tpu_custom_call" | custom-call | flops 100000000 | bytes 2000000 | tf_op jit(solution)/shard_map/pallas_call | solution.py:497
  (67 shorter events, 10.7 us)
Async XLA Ops:
  0.6 97.8 %copy-start = (bf16[128,128]{1,0:T(8,128)(2,1)S(1)}, bf16[128,128]{1,0:T(8,128)(2,1)}, u32[]{:S(2)}) copy-start(bf16[128,128]{1,0:T(8,128)(2,1)} %param.29) | copy-start | bytes 98308
  0.6 21.9 %copy-start.10 = (f32[3,512]{1,0:T(4,128)S(1)}, f32[3,512]{1,0:T(4,128)}, u32[]{:S(2)}) copy-start(f32[3,512]{1,0:T(4,128)} %frac.5) | copy-start | bytes 18436
  3.0 9.1 %collective-permute-start = (bf16[288,128]{1,0:T(8,128)(2,1)}, bf16[288,128]{1,0:T(8,128)(2,1)S(1)}, u32[]{:S(2)}, u32[]{:S(2)}) collective-permute-start(bf16[288,128]{1,0:T(8,128)(2,1)} %get-tuple-element.19), channel_id=1, source_target_pairs={{0,16},{16,32},{32,48},{48,64},{64,80},{80,96},{96,112},{112,0},{1... | collective-permute-start | bytes 221192 | tf_op jit(solution)/shard_map/ppermute | solution.py:413
  6.1 6.9 %collective-permute-start.1 = (bf16[288,128]{1,0:T(8,128)(2,1)}, bf16[288,128]{1,0:T(8,128)(2,1)S(1)}, u32[]{:S(2)}, u32[]{:S(2)}) collective-permute-start(bf16[288,128]{1,0:T(8,128)(2,1)} %get-tuple-element.19), channel_id=1, source_target_pairs={{16,0},{32,16},{48,32},{64,48},{80,64},{96,80},{112,96},{0,112},{1... | collective-permute-start | bytes 221192 | tf_op jit(solution)/shard_map/ppermute | solution.py:414
  13.1 6.0 %collective-permute-start.3 = (bf16[864,128]{1,0:T(8,128)(2,1)S(1)}, bf16[864,128]{1,0:T(8,128)(2,1)S(1)}, u32[]{:S(2)}, u32[]{:S(2)}) collective-permute-start(bf16[864,128]{1,0:T(8,128)(2,1)S(1)} %constant_dynamic-update-slice_fusion.x_own), channel_id=1, source_target_pairs={{1,0},{2,1},{3,2},{4,3},{5,4},{6,5},{7,6},{8,7},{9,8},{10,9},{11,1... | collective-permute-start | bytes 663560 | tf_op jit(solution)/shard_map/ppermute | solution.py:414
  14.8 7.8 %collective-permute-start.2 = (bf16[864,128]{1,0:T(8,128)(2,1)S(1)}, bf16[864,128]{1,0:T(8,128)(2,1)S(1)}, u32[]{:S(2)}, u32[]{:S(2)}) collective-permute-start(bf16[864,128]{1,0:T(8,128)(2,1)S(1)} %constant_dynamic-update-slice_fusion.x_own), channel_id=1, source_target_pairs={{0,1},{1,2},{2,3},{3,4},{4,5},{5,6},{6,7},{7,8},{8,9},{9,10},{10,1... | collective-permute-start | bytes 663560 | tf_op jit(solution)/shard_map/ppermute | solution.py:413
  41.0 8.2 %collective-permute-start.4 = (bf16[256,128]{1,0:T(8,128)(2,1)}, bf16[256,128]{1,0:T(8,128)(2,1)S(1)}, u32[]{:S(2)}, u32[]{:S(2)}) collective-permute-start(bf16[256,128]{1,0:T(8,128)(2,1)} %get-tuple-element.22), channel_id=1, source_target_pairs={{0,16},{16,32},{32,48},{48,64},{64,80},{80,96},{96,112},{112,0},{1... | collective-permute-start | bytes 196616 | tf_op jit(solution)/shard_map/ppermute | solution.py:413
  44.4 6.0 %collective-permute-start.5 = (bf16[256,128]{1,0:T(8,128)(2,1)}, bf16[256,128]{1,0:T(8,128)(2,1)S(1)}, u32[]{:S(2)}, u32[]{:S(2)}) collective-permute-start(bf16[256,128]{1,0:T(8,128)(2,1)} %get-tuple-element.22), channel_id=1, source_target_pairs={{16,0},{32,16},{48,32},{64,48},{80,64},{96,80},{112,96},{0,112},{1... | collective-permute-start | bytes 196616 | tf_op jit(solution)/shard_map/ppermute | solution.py:414
  50.4 7.4 %collective-permute-start.7 = (bf16[768,128]{1,0:T(8,128)(2,1)S(1)}, bf16[768,128]{1,0:T(8,128)(2,1)S(1)}, u32[]{:S(2)}, u32[]{:S(2)}) collective-permute-start(bf16[768,128]{1,0:T(8,128)(2,1)S(1)} %constant_dynamic-update-slice_fusion.3.x_own), channel_id=1, source_target_pairs={{1,0},{2,1},{3,2},{4,3},{5,4},{6,5},{7,6},{8,7},{9,8},{10,9},{11,1... | collective-permute-start | bytes 589832 | tf_op jit(solution)/shard_map/ppermute | solution.py:414
  50.5 7.3 %collective-permute-start.6 = (bf16[768,128]{1,0:T(8,128)(2,1)S(1)}, bf16[768,128]{1,0:T(8,128)(2,1)S(1)}, u32[]{:S(2)}, u32[]{:S(2)}) collective-permute-start(bf16[768,128]{1,0:T(8,128)(2,1)S(1)} %constant_dynamic-update-slice_fusion.3.x_own), channel_id=1, source_target_pairs={{0,1},{1,2},{2,3},{3,4},{4,5},{5,6},{6,7},{7,8},{8,9},{9,10},{10,1... | collective-permute-start | bytes 589832 | tf_op jit(solution)/shard_map/ppermute | solution.py:413
  57.8 41.9 %copy-start.11 = (bf16[16,128]{1,0:T(8,128)(2,1)S(1)}, bf16[16,128]{1,0:T(8,128)(2,1)}, u32[]{:S(2)}) copy-start(bf16[16,128]{1,0:T(8,128)(2,1)} %w_potential.1) | copy-start | bytes 12292
  57.8 41.9 %copy-start.13 = (f32[16]{0:T(128)S(1)}, f32[16]{0:T(128)}, u32[]{:S(2)}) copy-start(f32[16]{0:T(128)} %param.28) | copy-start | bytes 196
  57.8 41.9 %copy-start.14 = (bf16[128]{0:T(256)(128)(2,1)S(1)}, bf16[128]{0:T(256)(128)(2,1)}, u32[]{:S(2)}) copy-start(bf16[128]{0:T(256)(128)(2,1)} %param.31) | copy-start | bytes 772
  71.2 1.4 %collective-permute-start.8 = (bf16[64,384]{1,0:T(8,128)(2,1)}, bf16[64,384]{1,0:T(8,128)(2,1)S(1)}, u32[]{:S(2)}, u32[]{:S(2)}) collective-permute-start(bf16[64,384]{1,0:T(8,128)(2,1)} %get-tuple-element.30), channel_id=1, source_target_pairs={{0,1},{1,0},{2,3},{3,2},{4,5},{5,4},{6,7},{7,6},{8,9},{9,8},{10,11... | collective-permute-start | bytes 147464 | tf_op jit(solution)/shard_map/ppermute | solution.py:425
  73.5 5.4 %collective-permute-start.11 = (bf16[64,384]{1,0:T(8,128)(2,1)S(1)}, bf16[64,384]{1,0:T(8,128)(2,1)S(1)}, u32[]{:S(2)}, u32[]{:S(2)}) collective-permute-start(bf16[64,384]{1,0:T(8,128)(2,1)S(1)} %add_convert_fusion.3), channel_id=1, source_target_pairs={{0,18},{1,19},{2,16},{3,17},{4,22},{5,23},{6,20},{7,21},{8,26},{9,... | collective-permute-start | bytes 147464 | tf_op jit(solution)/shard_map/ppermute | solution.py:425
  74.9 6.1 %collective-permute-start.10 = (bf16[64,384]{1,0:T(8,128)(2,1)S(1)}, bf16[64,384]{1,0:T(8,128)(2,1)S(1)}, u32[]{:S(2)}, u32[]{:S(2)}) collective-permute-start(bf16[64,384]{1,0:T(8,128)(2,1)S(1)} %add_convert_fusion.3), channel_id=1, source_target_pairs={{0,16},{1,17},{2,18},{3,19},{4,20},{5,21},{6,22},{7,23},{8,24},{9,... | collective-permute-start | bytes 147464 | tf_op jit(solution)/shard_map/ppermute | solution.py:425
  75.8 5.2 %collective-permute-start.9 = (bf16[64,384]{1,0:T(8,128)(2,1)S(1)}, bf16[64,384]{1,0:T(8,128)(2,1)S(1)}, u32[]{:S(2)}, u32[]{:S(2)}) collective-permute-start(bf16[64,384]{1,0:T(8,128)(2,1)S(1)} %add_convert_fusion.3), channel_id=1, source_target_pairs={{0,2},{1,3},{2,0},{3,1},{4,6},{5,7},{6,4},{7,5},{8,10},{9,11},{10,... | collective-permute-start | bytes 147464 | tf_op jit(solution)/shard_map/ppermute | solution.py:425
  81.0 5.4 %collective-permute-start.14 = (bf16[64,384]{1,0:T(8,128)(2,1)S(1)}, bf16[64,384]{1,0:T(8,128)(2,1)S(1)}, u32[]{:S(2)}, u32[]{:S(2)}) collective-permute-start(bf16[64,384]{1,0:T(8,128)(2,1)S(1)} %add_convert_fusion.2), channel_id=1, source_target_pairs={{0,12},{1,13},{2,14},{3,15},{4,8},{5,9},{6,10},{7,11},{8,4},{9,5},... | collective-permute-start | bytes 147464 | tf_op jit(solution)/shard_map/ppermute | solution.py:425
  84.2 5.6 %collective-permute-start.13 = (bf16[64,384]{1,0:T(8,128)(2,1)S(1)}, bf16[64,384]{1,0:T(8,128)(2,1)S(1)}, u32[]{:S(2)}, u32[]{:S(2)}) collective-permute-start(bf16[64,384]{1,0:T(8,128)(2,1)S(1)} %add_convert_fusion.2), channel_id=1, source_target_pairs={{0,8},{1,9},{2,10},{3,11},{4,12},{5,13},{6,14},{7,15},{8,0},{9,1},... | collective-permute-start | bytes 147464 | tf_op jit(solution)/shard_map/ppermute | solution.py:425
  84.2 5.6 %collective-permute-start.12 = (bf16[64,384]{1,0:T(8,128)(2,1)S(1)}, bf16[64,384]{1,0:T(8,128)(2,1)S(1)}, u32[]{:S(2)}, u32[]{:S(2)}) collective-permute-start(bf16[64,384]{1,0:T(8,128)(2,1)S(1)} %add_convert_fusion.2), channel_id=1, source_target_pairs={{0,4},{1,5},{2,6},{3,7},{4,0},{5,1},{6,2},{7,3},{8,12},{9,13},{10,... | collective-permute-start | bytes 147464 | tf_op jit(solution)/shard_map/ppermute | solution.py:425
  89.8 5.4 %collective-permute-start.17 = (bf16[64,384]{1,0:T(8,128)(2,1)S(1)}, bf16[64,384]{1,0:T(8,128)(2,1)S(1)}, u32[]{:S(2)}, u32[]{:S(2)}) collective-permute-start(bf16[64,384]{1,0:T(8,128)(2,1)S(1)} %add_convert_fusion.1), channel_id=1, source_target_pairs={{0,96},{1,97},{2,98},{3,99},{4,100},{5,101},{6,102},{7,103},{8,104... | collective-permute-start | bytes 147464 | tf_op jit(solution)/shard_map/ppermute | solution.py:425
  92.7 5.6 %collective-permute-start.16 = (bf16[64,384]{1,0:T(8,128)(2,1)S(1)}, bf16[64,384]{1,0:T(8,128)(2,1)S(1)}, u32[]{:S(2)}, u32[]{:S(2)}) collective-permute-start(bf16[64,384]{1,0:T(8,128)(2,1)S(1)} %add_convert_fusion.1), channel_id=1, source_target_pairs={{0,64},{1,65},{2,66},{3,67},{4,68},{5,69},{6,70},{7,71},{8,72},{9,... | collective-permute-start | bytes 147464 | tf_op jit(solution)/shard_map/ppermute | solution.py:425
  93.6 4.7 %collective-permute-start.15 = (bf16[64,384]{1,0:T(8,128)(2,1)S(1)}, bf16[64,384]{1,0:T(8,128)(2,1)S(1)}, u32[]{:S(2)}, u32[]{:S(2)}) collective-permute-start(bf16[64,384]{1,0:T(8,128)(2,1)S(1)} %add_convert_fusion.1), channel_id=1, source_target_pairs={{0,32},{1,33},{2,34},{3,35},{4,36},{5,37},{6,38},{7,39},{8,40},{9,... | collective-permute-start | bytes 147464 | tf_op jit(solution)/shard_map/ppermute | solution.py:425
  98.3 1.3 %collective-permute-start.18 = (bf16[64,384]{1,0:T(8,128)(2,1)S(1)}, bf16[64,384]{1,0:T(8,128)(2,1)S(1)}, u32[]{:S(2)}, u32[]{:S(2)}) collective-permute-start(bf16[64,384]{1,0:T(8,128)(2,1)S(1)} %add_convert_fusion.own_half), channel_id=1, source_target_pairs={{0,1},{1,0},{2,3},{3,2},{4,5},{5,4},{6,7},{7,6},{8,9},{9,8},{10,11... | collective-permute-start | bytes 147464 | tf_op jit(solution)/shard_map/ppermute | solution.py:425
  (13 other events, 191.7 us)

commit v4 on v3

--- a/solution.py
+++ b/solution.py
@@ -417,7 +417,7 @@
     return near(low), near(block), near(high)
 
 
-RINGS = ((2, 16, 18), (4, 8, 12), (32, 64, 96))
+RINGS = ((4, 8, 12), (32, 64, 96), (2, 16, 18))
 
 
 def exchange(part, offset):

time: 103 us -> 103 us (level)
    ppermute x11, starting transfers between devices: 12.6 us -> 13.7 us  [exchange(): lax.ppermute(part, ('gx', 'yz'), [(i, i ^ offset) for i in range(count)])]
    ppermute x11, waiting for transfers between devices: 13.7 us -> 12.7 us  [exchange(): lax.ppermute(part, ('gx', 'yz'), [(i, i ^ offset) for i in range(count)])]
where the time goes in v4:
time: 103 us; the launch traced here: 101 us
  Pallas kernels  44.4 us (43%)
  starting transfers between devices  28.3 us (27%)
  waiting for transfers between devices  23.6 us (23%)
  local copies, waits for them, and re-layouts  1.87 us (2%)
  matrix products  1.07 us (1%)
    pallas_call x1, Pallas kernels, shards(): call(layer_kernel, [pl.BlockSpec(memory_space=pl.ANY), SMEM] + [VMEM] * 1...  18.4 us
    ppermute x11, starting transfers between devices, exchange(): lax.ppermute(part, ('gx', 'yz'), [(i, i ^ offset) for i in range(count)])  13.7 us
    pallas_call x1, Pallas kernels, shards(): pl.pallas_call(last_layer_kernel, grid=(4,), out_shape=(shape(T, C, dtype...  13.4 us
    ppermute x11, waiting for transfers between devices, exchange(): lax.ppermute(part, ('gx', 'yz'), [(i, i ^ offset) for i in range(count)])  12.7 us
    ppermute x4, waiting for transfers between devices, halo(): low = lax.ppermute(block, axis, forward)  8.33 us
    ppermute x4, starting transfers between devices, halo(): high = lax.ppermute(block, axis, backward)  7.57 us
    ppermute x4, starting transfers between devices, halo(): low = lax.ppermute(block, axis, forward)  7.07 us
    pallas_call x1, Pallas kernels, shards(): pl.pallas_call(filter_kernel, grid=(4,), out_shape=shape(8, 2, T, 2 * C,...  6.75 us
  transfers between devices with their start and end apart: 19, of which 13 were waited for; matrix products, arithmetic and copies ran while one was open for 3% of the time, Pallas kernels for 9%

profile of v4, /device:TPU:0, one launch (start us, length us, event | category | flops | bytes accessed | tf_op | source)
XLA Modules:
  0.0 101.0 jit_solution(13377260840251554633)
XLA Ops:
  0.7 2.3 %shard_map.176 = (bf16[512,128]{1,0:T(8,128)(2,1)}, bf16[288,128]{1,0:T(8,128)(2,1)}) custom-call(s32[256]{0:T(256)} %send.3, s32[2,128]{1,0:T(2,128)} %bitcast.14, bf16[512,128]{1,0:T(8,128)(2,1)} %state.1, f32[3,512]{1,0:T(4,128)} %frac.5, bf16[2,128,128]{2,1,0:T(8,128)(2,1)} %w_in.3), custom_call_target="tpu_custom_call" | custom-call | flops 20000000 | bytes 300000 | tf_op jit(solution)/shard_map/pallas_call | solution.py:443
  3.0 3.1 %collective-permute-start = (bf16[288,128]{1,0:T(8,128)(2,1)}, bf16[288,128]{1,0:T(8,128)(2,1)S(1)}, u32[]{:S(2)}, u32[]{:S(2)}) collective-permute-start(bf16[288,128]{1,0:T(8,128)(2,1)} %get-tuple-element.19), channel_id=1, source_target_pairs={{0,16},{16,32},{32,48},{48,64},{64,80},{80,96},{96,112},{112,0},{1... | collective-permute-start | bytes 221192 | tf_op jit(solution)/shard_map/ppermute | solution.py:413
  6.1 3.5 %collective-permute-start.1 = (bf16[288,128]{1,0:T(8,128)(2,1)}, bf16[288,128]{1,0:T(8,128)(2,1)S(1)}, u32[]{:S(2)}, u32[]{:S(2)}) collective-permute-start(bf16[288,128]{1,0:T(8,128)(2,1)} %get-tuple-element.19), channel_id=1, source_target_pairs={{16,0},{32,16},{48,32},{64,48},{80,64},{96,80},{112,96},{0,112},{1... | collective-permute-start | bytes 221192 | tf_op jit(solution)/shard_map/ppermute | solution.py:414
  9.7 2.5 %collective-permute-done = bf16[288,128]{1,0:T(8,128)(2,1)S(1)} collective-permute-done((bf16[288,128]{1,0:T(8,128)(2,1)}, bf16[288,128]{1,0:T(8,128)(2,1)S(1)}, u32[]{:S(2)}, u32[]{:S(2)}) %collective-permute-start) | collective-permute-done | bytes 73760 | tf_op jit(solution)/shard_map/ppermute | solution.py:413
  13.1 1.7 %collective-permute-start.3 = (bf16[864,128]{1,0:T(8,128)(2,1)S(1)}, bf16[864,128]{1,0:T(8,128)(2,1)S(1)}, u32[]{:S(2)}, u32[]{:S(2)}) collective-permute-start(bf16[864,128]{1,0:T(8,128)(2,1)S(1)} %constant_dynamic-update-slice_fusion.x_own), channel_id=1, source_target_pairs={{1,0},{2,1},{3,2},{4,3},{5,4},{6,5},{7,6},{8,7},{9,8},{10,9},{11,1... | collective-permute-start | bytes 663560 | tf_op jit(solution)/shard_map/ppermute | solution.py:414
  14.8 2.2 %shard_map.175 = (s32[128,128]{1,0:T(8,128)}, bf16[352,1024]{1,0:T(8,128)(2,1)}, f32[16,512]{1,0:T(8,128)}, f32[16,384]{1,0:T(8,128)}) custom-call(s32[32,512]{1,0:T(8,128)} %neighbours.1, s32[32,512]{1,0:T(8,128)} %mask.1, f32[3,512]{1,0:T(4,128)} %frac.5, s32[3,32]{1,0:T(4,128)} %waves.1), custom_call_target="tpu_custom_call" | custom-call | flops 2000000000 | bytes 4000000 | tf_op jit(solution)/shard_map/pallas_call | solution.py:448
  17.0 2.1 %collective-permute-done.3.x_high = bf16[864,128]{1,0:T(8,128)(2,1)S(1)} collective-permute-done((bf16[864,128]{1,0:T(8,128)(2,1)S(1)}, bf16[864,128]{1,0:T(8,128)(2,1)S(1)}, u32[]{:S(2)}, u32[]{:S(2)}) %collective-permute-start.3) | collective-permute-done | bytes 221216 | tf_op jit(solution)/shard_map/ppermute | solution.py:414
  19.1 3.4 %collective-permute-done.2.x_low = bf16[864,128]{1,0:T(8,128)(2,1)S(1)} collective-permute-done((bf16[864,128]{1,0:T(8,128)(2,1)S(1)}, bf16[864,128]{1,0:T(8,128)(2,1)S(1)}, u32[]{:S(2)}, u32[]{:S(2)}) %collective-permute-start.2) | collective-permute-done | bytes 221216 | tf_op jit(solution)/shard_map/ppermute | solution.py:413
  22.6 18.4 %shard_map.177 = (bf16[512,128]{1,0:T(8,128)(2,1)}, bf16[512,128]{1,0:T(8,128)(2,1)}, bf16[256,128]{1,0:T(8,128)(2,1)}, f32[128,128]{1,0:T(8,128)}) custom-call(s32[16384]{0:T(1024)} %bitcast.12, s32[256]{0:T(256)} %send.3, s32[128,128]{1,0:T(8,128)} %get-tuple-element.18.slots, f32[3,512]{1,0:T(4,128)S(1)} %copy-done.10, ...), custom_call_target="tpu_custom_call" | custom-call | flops 4000000000 | bytes 4000000 | tf_op jit(solution)/shard_map/pallas_call | solution.py:454
  41.0 3.4 %collective-permute-start.4 = (bf16[256,128]{1,0:T(8,128)(2,1)}, bf16[256,128]{1,0:T(8,128)(2,1)S(1)}, u32[]{:S(2)}, u32[]{:S(2)}) collective-permute-start(bf16[256,128]{1,0:T(8,128)(2,1)} %get-tuple-element.22), channel_id=1, source_target_pairs={{0,16},{16,32},{32,48},{48,64},{64,80},{80,96},{96,112},{112,0},{1... | collective-permute-start | bytes 196616 | tf_op jit(solution)/shard_map/ppermute | solution.py:413
  44.4 2.3 %collective-permute-start.5 = (bf16[256,128]{1,0:T(8,128)(2,1)}, bf16[256,128]{1,0:T(8,128)(2,1)S(1)}, u32[]{:S(2)}, u32[]{:S(2)}) collective-permute-start(bf16[256,128]{1,0:T(8,128)(2,1)} %get-tuple-element.22), channel_id=1, source_target_pairs={{16,0},{32,16},{48,32},{64,48},{80,64},{96,80},{112,96},{0,112},{1... | collective-permute-start | bytes 196616 | tf_op jit(solution)/shard_map/ppermute | solution.py:414
  46.7 2.4 %collective-permute-done.4 = bf16[256,128]{1,0:T(8,128)(2,1)S(1)} collective-permute-done((bf16[256,128]{1,0:T(8,128)(2,1)}, bf16[256,128]{1,0:T(8,128)(2,1)S(1)}, u32[]{:S(2)}, u32[]{:S(2)}) %collective-permute-start.4) | collective-permute-done | bytes 65568 | tf_op jit(solution)/shard_map/ppermute | solution.py:413
  51.0 6.8 %shard_map.178.filters = bf16[8,2,512,256]{3,2,1,0:T(8,128)(2,1)} custom-call(f32[128,128]{1,0:T(8,128)} %get-tuple-element.21.chord, bf16[2,32,128]{2,1,0:T(8,128)(2,1)} %w1.3, bf16[2,128,128]{2,1,0:T(8,128)(2,1)} %w2.3), custom_call_target="tpu_custom_call" | custom-call | flops 4000000000 | bytes 8000000 | tf_op jit(solution)/shard_map/pallas_call | solution.py:471
  57.8 13.4 %shard_map.179 = (bf16[512,128]{1,0:T(8,128)(2,1)}, bf16[64,384]{1,0:T(8,128)(2,1)}, bf16[64,384]{1,0:T(8,128)(2,1)}) custom-call(s32[16384]{0:T(1024)} %bitcast.13, s32[1]{0:T(128)} %bitcast.1.core, bf16[8,2,512,256]{3,2,1,0:T(8,128)(2,1)} %shard_map.178.filters, bf16[768,128]{1,0:T(8,128)(2,1)S(1)} %collective-permute-done.6.x_low, ...), custom_call_target="tpu_custom_call" | custom-call | flops 1000000000 | bytes 8000000 | tf_op jit(solution)/shard_map/pallas_call | solution.py:484
  71.3 1.4 %collective-permute-done.8 = bf16[64,384]{1,0:T(8,128)(2,1)S(1)} collective-permute-done((bf16[64,384]{1,0:T(8,128)(2,1)}, bf16[64,384]{1,0:T(8,128)(2,1)S(1)}, u32[]{:S(2)}, u32[]{:S(2)}) %collective-permute-start.8) | collective-permute-done | bytes 49184 | tf_op jit(solution)/shard_map/ppermute | solution.py:425
  75.7 1.9 %collective-permute-start.9 = (bf16[64,384]{1,0:T(8,128)(2,1)S(1)}, bf16[64,384]{1,0:T(8,128)(2,1)S(1)}, u32[]{:S(2)}, u32[]{:S(2)}) collective-permute-start(bf16[64,384]{1,0:T(8,128)(2,1)S(1)} %add_convert_fusion.3), channel_id=1, source_target_pairs={{0,4},{1,5},{2,6},{3,7},{4,0},{5,1},{6,2},{7,3},{8,12},{9,13},{10,... | collective-permute-start | bytes 147464 | tf_op jit(solution)/shard_map/ppermute | solution.py:425
  77.7 1.7 %collective-permute-done.11 = bf16[64,384]{1,0:T(8,128)(2,1)S(1)} collective-permute-done((bf16[64,384]{1,0:T(8,128)(2,1)S(1)}, bf16[64,384]{1,0:T(8,128)(2,1)S(1)}, u32[]{:S(2)}, u32[]{:S(2)}) %collective-permute-start.11) | collective-permute-done | bytes 49184 | tf_op jit(solution)/shard_map/ppermute | solution.py:425
  80.5 2.4 %collective-permute-start.14 = (bf16[64,384]{1,0:T(8,128)(2,1)S(1)}, bf16[64,384]{1,0:T(8,128)(2,1)S(1)}, u32[]{:S(2)}, u32[]{:S(2)}) collective-permute-start(bf16[64,384]{1,0:T(8,128)(2,1)S(1)} %add_convert_fusion.2), channel_id=1, source_target_pairs={{0,96},{1,97},{2,98},{3,99},{4,100},{5,101},{6,102},{7,103},{8,104... | collective-permute-start | bytes 147464 | tf_op jit(solution)/shard_map/ppermute | solution.py:425
  83.0 1.4 %collective-permute-start.13 = (bf16[64,384]{1,0:T(8,128)(2,1)S(1)}, bf16[64,384]{1,0:T(8,128)(2,1)S(1)}, u32[]{:S(2)}, u32[]{:S(2)}) collective-permute-start(bf16[64,384]{1,0:T(8,128)(2,1)S(1)} %add_convert_fusion.2), channel_id=1, source_target_pairs={{0,64},{1,65},{2,66},{3,67},{4,68},{5,69},{6,70},{7,71},{8,72},{9,... | collective-permute-start | bytes 147464 | tf_op jit(solution)/shard_map/ppermute | solution.py:425
  84.7 1.7 %collective-permute-done.14 = bf16[64,384]{1,0:T(8,128)(2,1)S(1)} collective-permute-done((bf16[64,384]{1,0:T(8,128)(2,1)S(1)}, bf16[64,384]{1,0:T(8,128)(2,1)S(1)}, u32[]{:S(2)}, u32[]{:S(2)}) %collective-permute-start.14) | collective-permute-done | bytes 49184 | tf_op jit(solution)/shard_map/ppermute | solution.py:425
  86.5 2.1 %collective-permute-done.13 = bf16[64,384]{1,0:T(8,128)(2,1)S(1)} collective-permute-done((bf16[64,384]{1,0:T(8,128)(2,1)S(1)}, bf16[64,384]{1,0:T(8,128)(2,1)S(1)}, u32[]{:S(2)}, u32[]{:S(2)}) %collective-permute-start.13) | collective-permute-done | bytes 49184 | tf_op jit(solution)/shard_map/ppermute | solution.py:425
  88.6 4.1 %collective-permute-start.17 = (bf16[64,384]{1,0:T(8,128)(2,1)S(1)}, bf16[64,384]{1,0:T(8,128)(2,1)S(1)}, u32[]{:S(2)}, u32[]{:S(2)}) collective-permute-start(bf16[64,384]{1,0:T(8,128)(2,1)S(1)} %add_convert_fusion.1), channel_id=1, source_target_pairs={{0,18},{1,19},{2,16},{3,17},{4,22},{5,23},{6,20},{7,21},{8,26},{9,... | collective-permute-start | bytes 147464 | tf_op jit(solution)/shard_map/ppermute | solution.py:425
  94.9 3.4 %collective-permute-done.16 = bf16[64,384]{1,0:T(8,128)(2,1)S(1)} collective-permute-done((bf16[64,384]{1,0:T(8,128)(2,1)S(1)}, bf16[64,384]{1,0:T(8,128)(2,1)S(1)}, u32[]{:S(2)}, u32[]{:S(2)}) %collective-permute-start.16) | collective-permute-done | bytes 49184 | tf_op jit(solution)/shard_map/ppermute | solution.py:425
  99.6 1.3 %shard_map.180 = (f32[16,512]{1,0:T(8,128)}, f32[1,512]{1,0:T(1,128)}) custom-call(s32[1]{0:T(128)} %bitcast.1.core, bf16[64,384]{1,0:T(8,128)(2,1)S(1)} %add_convert_fusion.own_half, bf16[64,384]{1,0:T(8,128)(2,1)S(1)} %collective-permute-done.18.other_half, bf16[352,1024]{1,0:T(8,128)(2,1)S(1)} %copy-done.1, f32[16,512]{1,0:T(8,128)S(1)} %copy-done.2, ...), custom_call_target="tpu_custom_call" | custom-call | flops 100000000 | bytes 2000000 | tf_op jit(solution)/shard_map/pallas_call | solution.py:497
  (67 shorter events, 11.0 us)
Async XLA Ops:
  0.6 97.8 %copy-start = (bf16[128,128]{1,0:T(8,128)(2,1)S(1)}, bf16[128,128]{1,0:T(8,128)(2,1)}, u32[]{:S(2)}) copy-start(bf16[128,128]{1,0:T(8,128)(2,1)} %param.29) | copy-start | bytes 98308
  0.6 21.9 %copy-start.10 = (f32[3,512]{1,0:T(4,128)S(1)}, f32[3,512]{1,0:T(4,128)}, u32[]{:S(2)}) copy-start(f32[3,512]{1,0:T(4,128)} %frac.5) | copy-start | bytes 18436
  3.0 9.1 %collective-permute-start = (bf16[288,128]{1,0:T(8,128)(2,1)}, bf16[288,128]{1,0:T(8,128)(2,1)S(1)}, u32[]{:S(2)}, u32[]{:S(2)}) collective-permute-start(bf16[288,128]{1,0:T(8,128)(2,1)} %get-tuple-element.19), channel_id=1, source_target_pairs={{0,16},{16,32},{32,48},{48,64},{64,80},{80,96},{96,112},{112,0},{1... | collective-permute-start | bytes 221192 | tf_op jit(solution)/shard_map/ppermute | solution.py:413
  6.1 6.9 %collective-permute-start.1 = (bf16[288,128]{1,0:T(8,128)(2,1)}, bf16[288,128]{1,0:T(8,128)(2,1)S(1)}, u32[]{:S(2)}, u32[]{:S(2)}) collective-permute-start(bf16[288,128]{1,0:T(8,128)(2,1)} %get-tuple-element.19), channel_id=1, source_target_pairs={{16,0},{32,16},{48,32},{64,48},{80,64},{96,80},{112,96},{0,112},{1... | collective-permute-start | bytes 221192 | tf_op jit(solution)/shard_map/ppermute | solution.py:414
  13.1 6.0 %collective-permute-start.3 = (bf16[864,128]{1,0:T(8,128)(2,1)S(1)}, bf16[864,128]{1,0:T(8,128)(2,1)S(1)}, u32[]{:S(2)}, u32[]{:S(2)}) collective-permute-start(bf16[864,128]{1,0:T(8,128)(2,1)S(1)} %constant_dynamic-update-slice_fusion.x_own), channel_id=1, source_target_pairs={{1,0},{2,1},{3,2},{4,3},{5,4},{6,5},{7,6},{8,7},{9,8},{10,9},{11,1... | collective-permute-start | bytes 663560 | tf_op jit(solution)/shard_map/ppermute | solution.py:414
  14.8 7.8 %collective-permute-start.2 = (bf16[864,128]{1,0:T(8,128)(2,1)S(1)}, bf16[864,128]{1,0:T(8,128)(2,1)S(1)}, u32[]{:S(2)}, u32[]{:S(2)}) collective-permute-start(bf16[864,128]{1,0:T(8,128)(2,1)S(1)} %constant_dynamic-update-slice_fusion.x_own), channel_id=1, source_target_pairs={{0,1},{1,2},{2,3},{3,4},{4,5},{5,6},{6,7},{7,8},{8,9},{9,10},{10,1... | collective-permute-start | bytes 663560 | tf_op jit(solution)/shard_map/ppermute | solution.py:413
  41.0 8.2 %collective-permute-start.4 = (bf16[256,128]{1,0:T(8,128)(2,1)}, bf16[256,128]{1,0:T(8,128)(2,1)S(1)}, u32[]{:S(2)}, u32[]{:S(2)}) collective-permute-start(bf16[256,128]{1,0:T(8,128)(2,1)} %get-tuple-element.22), channel_id=1, source_target_pairs={{0,16},{16,32},{32,48},{48,64},{64,80},{80,96},{96,112},{112,0},{1... | collective-permute-start | bytes 196616 | tf_op jit(solution)/shard_map/ppermute | solution.py:413
  44.4 6.0 %collective-permute-start.5 = (bf16[256,128]{1,0:T(8,128)(2,1)}, bf16[256,128]{1,0:T(8,128)(2,1)S(1)}, u32[]{:S(2)}, u32[]{:S(2)}) collective-permute-start(bf16[256,128]{1,0:T(8,128)(2,1)} %get-tuple-element.22), channel_id=1, source_target_pairs={{16,0},{32,16},{48,32},{64,48},{80,64},{96,80},{112,96},{0,112},{1... | collective-permute-start | bytes 196616 | tf_op jit(solution)/shard_map/ppermute | solution.py:414
  50.4 7.4 %collective-permute-start.7 = (bf16[768,128]{1,0:T(8,128)(2,1)S(1)}, bf16[768,128]{1,0:T(8,128)(2,1)S(1)}, u32[]{:S(2)}, u32[]{:S(2)}) collective-permute-start(bf16[768,128]{1,0:T(8,128)(2,1)S(1)} %constant_dynamic-update-slice_fusion.3.x_own), channel_id=1, source_target_pairs={{1,0},{2,1},{3,2},{4,3},{5,4},{6,5},{7,6},{8,7},{9,8},{10,9},{11,1... | collective-permute-start | bytes 589832 | tf_op jit(solution)/shard_map/ppermute | solution.py:414
  50.5 7.3 %collective-permute-start.6 = (bf16[768,128]{1,0:T(8,128)(2,1)S(1)}, bf16[768,128]{1,0:T(8,128)(2,1)S(1)}, u32[]{:S(2)}, u32[]{:S(2)}) collective-permute-start(bf16[768,128]{1,0:T(8,128)(2,1)S(1)} %constant_dynamic-update-slice_fusion.3.x_own), channel_id=1, source_target_pairs={{0,1},{1,2},{2,3},{3,4},{4,5},{5,6},{6,7},{7,8},{8,9},{9,10},{10,1... | collective-permute-start | bytes 589832 | tf_op jit(solution)/shard_map/ppermute | solution.py:413
  57.8 41.9 %copy-start.11 = (bf16[16,128]{1,0:T(8,128)(2,1)S(1)}, bf16[16,128]{1,0:T(8,128)(2,1)}, u32[]{:S(2)}) copy-start(bf16[16,128]{1,0:T(8,128)(2,1)} %w_potential.1) | copy-start | bytes 12292
  57.8 41.9 %copy-start.13 = (f32[16]{0:T(128)S(1)}, f32[16]{0:T(128)}, u32[]{:S(2)}) copy-start(f32[16]{0:T(128)} %param.28) | copy-start | bytes 196
  57.8 41.9 %copy-start.14 = (bf16[128]{0:T(256)(128)(2,1)S(1)}, bf16[128]{0:T(256)(128)(2,1)}, u32[]{:S(2)}) copy-start(bf16[128]{0:T(256)(128)(2,1)} %param.31) | copy-start | bytes 772
  71.2 1.4 %collective-permute-start.8 = (bf16[64,384]{1,0:T(8,128)(2,1)}, bf16[64,384]{1,0:T(8,128)(2,1)S(1)}, u32[]{:S(2)}, u32[]{:S(2)}) collective-permute-start(bf16[64,384]{1,0:T(8,128)(2,1)} %get-tuple-element.30), channel_id=1, source_target_pairs={{0,1},{1,0},{2,3},{3,2},{4,5},{5,4},{6,7},{7,6},{8,9},{9,8},{10,11... | collective-permute-start | bytes 147464 | tf_op jit(solution)/shard_map/ppermute | solution.py:425
  73.5 5.9 %collective-permute-start.11 = (bf16[64,384]{1,0:T(8,128)(2,1)S(1)}, bf16[64,384]{1,0:T(8,128)(2,1)S(1)}, u32[]{:S(2)}, u32[]{:S(2)}) collective-permute-start(bf16[64,384]{1,0:T(8,128)(2,1)S(1)} %add_convert_fusion.3), channel_id=1, source_target_pairs={{0,12},{1,13},{2,14},{3,15},{4,8},{5,9},{6,10},{7,11},{8,4},{9,5},... | collective-permute-start | bytes 147464 | tf_op jit(solution)/shard_map/ppermute | solution.py:425
  74.5 6.0 %collective-permute-start.10 = (bf16[64,384]{1,0:T(8,128)(2,1)S(1)}, bf16[64,384]{1,0:T(8,128)(2,1)S(1)}, u32[]{:S(2)}, u32[]{:S(2)}) collective-permute-start(bf16[64,384]{1,0:T(8,128)(2,1)S(1)} %add_convert_fusion.3), channel_id=1, source_target_pairs={{0,8},{1,9},{2,10},{3,11},{4,12},{5,13},{6,14},{7,15},{8,0},{9,1},... | collective-permute-start | bytes 147464 | tf_op jit(solution)/shard_map/ppermute | solution.py:425
  75.7 4.8 %collective-permute-start.9 = (bf16[64,384]{1,0:T(8,128)(2,1)S(1)}, bf16[64,384]{1,0:T(8,128)(2,1)S(1)}, u32[]{:S(2)}, u32[]{:S(2)}) collective-permute-start(bf16[64,384]{1,0:T(8,128)(2,1)S(1)} %add_convert_fusion.3), channel_id=1, source_target_pairs={{0,4},{1,5},{2,6},{3,7},{4,0},{5,1},{6,2},{7,3},{8,12},{9,13},{10,... | collective-permute-start | bytes 147464 | tf_op jit(solution)/shard_map/ppermute | solution.py:425
  80.5 5.9 %collective-permute-start.14 = (bf16[64,384]{1,0:T(8,128)(2,1)S(1)}, bf16[64,384]{1,0:T(8,128)(2,1)S(1)}, u32[]{:S(2)}, u32[]{:S(2)}) collective-permute-start(bf16[64,384]{1,0:T(8,128)(2,1)S(1)} %add_convert_fusion.2), channel_id=1, source_target_pairs={{0,96},{1,97},{2,98},{3,99},{4,100},{5,101},{6,102},{7,103},{8,104... | collective-permute-start | bytes 147464 | tf_op jit(solution)/shard_map/ppermute | solution.py:425
  83.0 5.6 %collective-permute-start.13 = (bf16[64,384]{1,0:T(8,128)(2,1)S(1)}, bf16[64,384]{1,0:T(8,128)(2,1)S(1)}, u32[]{:S(2)}, u32[]{:S(2)}) collective-permute-start(bf16[64,384]{1,0:T(8,128)(2,1)S(1)} %add_convert_fusion.2), channel_id=1, source_target_pairs={{0,64},{1,65},{2,66},{3,67},{4,68},{5,69},{6,70},{7,71},{8,72},{9,... | collective-permute-start | bytes 147464 | tf_op jit(solution)/shard_map/ppermute | solution.py:425
  84.4 4.2 %collective-permute-start.12 = (bf16[64,384]{1,0:T(8,128)(2,1)S(1)}, bf16[64,384]{1,0:T(8,128)(2,1)S(1)}, u32[]{:S(2)}, u32[]{:S(2)}) collective-permute-start(bf16[64,384]{1,0:T(8,128)(2,1)S(1)} %add_convert_fusion.2), channel_id=1, source_target_pairs={{0,32},{1,33},{2,34},{3,35},{4,36},{5,37},{6,38},{7,39},{8,40},{9,... | collective-permute-start | bytes 147464 | tf_op jit(solution)/shard_map/ppermute | solution.py:425
  88.6 6.3 %collective-permute-start.17 = (bf16[64,384]{1,0:T(8,128)(2,1)S(1)}, bf16[64,384]{1,0:T(8,128)(2,1)S(1)}, u32[]{:S(2)}, u32[]{:S(2)}) collective-permute-start(bf16[64,384]{1,0:T(8,128)(2,1)S(1)} %add_convert_fusion.1), channel_id=1, source_target_pairs={{0,18},{1,19},{2,16},{3,17},{4,22},{5,23},{6,20},{7,21},{8,26},{9,... | collective-permute-start | bytes 147464 | tf_op jit(solution)/shard_map/ppermute | solution.py:425
  92.7 5.6 %collective-permute-start.16 = (bf16[64,384]{1,0:T(8,128)(2,1)S(1)}, bf16[64,384]{1,0:T(8,128)(2,1)S(1)}, u32[]{:S(2)}, u32[]{:S(2)}) collective-permute-start(bf16[64,384]{1,0:T(8,128)(2,1)S(1)} %add_convert_fusion.1), channel_id=1, source_target_pairs={{0,16},{1,17},{2,18},{3,19},{4,20},{5,21},{6,22},{7,23},{8,24},{9,... | collective-permute-start | bytes 147464 | tf_op jit(solution)/shard_map/ppermute | solution.py:425
  93.8 4.5 %collective-permute-start.15 = (bf16[64,384]{1,0:T(8,128)(2,1)S(1)}, bf16[64,384]{1,0:T(8,128)(2,1)S(1)}, u32[]{:S(2)}, u32[]{:S(2)}) collective-permute-start(bf16[64,384]{1,0:T(8,128)(2,1)S(1)} %add_convert_fusion.1), channel_id=1, source_target_pairs={{0,2},{1,3},{2,0},{3,1},{4,6},{5,7},{6,4},{7,5},{8,10},{9,11},{10,... | collective-permute-start | bytes 147464 | tf_op jit(solution)/shard_map/ppermute | solution.py:425
  98.3 1.3 %collective-permute-start.18 = (bf16[64,384]{1,0:T(8,128)(2,1)S(1)}, bf16[64,384]{1,0:T(8,128)(2,1)S(1)}, u32[]{:S(2)}, u32[]{:S(2)}) collective-permute-start(bf16[64,384]{1,0:T(8,128)(2,1)S(1)} %add_convert_fusion.own_half), channel_id=1, source_target_pairs={{0,1},{1,0},{2,3},{3,2},{4,5},{5,4},{6,7},{7,6},{8,9},{9,8},{10,11... | collective-permute-start | bytes 147464 | tf_op jit(solution)/shard_map/ppermute | solution.py:425
  (13 other events, 191.6 us)
